TPU v7x, 512 devices: a whole 4x4x16 slice. The times are simulated.
512 devices in a mesh: ctx: 8 (over y, z_hi), tp: 64 (over x, z_lo, core).
Axes of the slice: x: 4, y: 4, z: 16 (z_hi: 2, z_lo: 8; z = z_hi * 8 + z_lo), core: 2. Of those that a mesh axis runs over, the one named last changes fastest.
Arguments:
- hidden: bfloat16 [2048, 2048], P(('ctx', 'tp')), may hold values from -6 to 6
- w_in: bfloat16 [2048, 8192], P(None, 'tp'), may hold values from -0.125 to 0.125
- w_bc: bfloat16 [2048, 32], replicated, may hold values from -0.125 to 0.125
- w_dt: bfloat16 [64, 2048], P('tp'), may hold values from -0.125 to 0.125
- dt_bias: float32 [64], P('tp'), may hold values from -5 to -3
- a_log: float32 [64], P('tp'), may hold values from -4.6 to 0
- d_skip: float32 [64], P('tp'), may hold values from 0.5 to 1.5
- conv_w: float32 [4, 4096], P(None, 'tp'), may hold values from -3 to 3
- w_out: bfloat16 [4096, 2048], P('tp'), may hold values from -0.09375 to 0.09375
- d_out: bfloat16 [2048, 2048], P(('ctx', 'tp')), may hold values from -6 to 6
Outputs:
- d_hidden: bfloat16 [2048, 2048], P(('ctx', 'tp'))
- d_w_in: float32 [2048, 8192], P(None, 'tp')
- d_w_out: float32 [4096, 2048], P('tp')
- d_w_bc: float32 [2048, 32], replicated
All inputs are finite; a program needn't handle non-finite values.
Results may differ from a plain program's by a relative error of at most 0.017.
Values may be sent and summed in bfloat16 or wider, within the bound.
A program may use at most 64 MiB of HBM per device.

v0:
```python
import math

import jax
import jax.numpy as jnp
from jax import lax
from jax.sharding import PartitionSpec as P

STATE = 16
CONV = 4


precise = lax.Precision.HIGHEST


def padded(array, sides, width):
    for axis, dim in sides:
        size, length = (lax.axis_size(axis), array.shape[dim])
        up = [(i, (i + 1) % size) for i in range(size - 1)]
        down = [(j, i) for i, j in up]
        last = lax.slice_in_dim(array, length - width, length, axis=dim)
        leading = lax.slice_in_dim(array, 0, width, axis=dim)
        before = lax.ppermute(last, axis, up)
        after = lax.ppermute(leading, axis, down)
        array = jnp.concatenate([before, array, after], axis=dim)
    return array


def entering(array, axis, combine, identity, reverse):
    length, index = (lax.axis_size(axis), lax.axis_index(axis))
    everything = jax.tree.map(lambda part: lax.all_gather(part, axis), array)
    start = jax.tree.map(
        lambda part, zero: jnp.broadcast_to(jnp.asarray(zero, part.dtype), part.shape),
        array,
        identity,
    )

    def step(k, before):
        at = length - 1 - k if reverse else k
        reached = at > index if reverse else at < index
        new = combine(before, jax.tree.map(lambda part: part[at], everything))
        return jax.tree.map(lambda a, b: jnp.where(reached, a, b), new, before)

    return lax.fori_loop(0, length, step, start)


def times_rows(operand_a, operand_b):
    return lax.dot_general(
        operand_a, operand_b, (((1,), (1,)), ((), ())), preferred_element_type=jnp.float32
    )


def across_rows(operand_a, operand_b):
    return lax.dot_general(
        operand_a, operand_b, (((0,), (0,)), ((), ())), preferred_element_type=jnp.float32
    )


def conv_silu(x_ext, conv_w):
    length = x_ext.shape[0] - CONV + 1
    summed = conv_w[0] * x_ext[0:length]
    for shift_k in range(1, CONV):
        summed = summed + conv_w[shift_k] * x_ext[shift_k : shift_k + length]
    return jax.nn.silu(summed)


def block_ssd(conv_out, steps_dt, b_rows, c_rows, decay_rate, state_in):
    positions = conv_out.shape[0]
    log_keep = jnp.cumsum(steps_dt * decay_rate)
    causal = lax.broadcasted_iota(jnp.int32, (positions, positions), 0) >= lax.broadcasted_iota(
        jnp.int32, (positions, positions), 1
    )
    decays = jnp.exp(jnp.where(causal, log_keep[:, None] - log_keep[None, :], -jnp.inf))
    scores = jnp.einsum("in,jn->ij", c_rows, b_rows, precision=precise) * decays
    weighted = steps_dt[:, None] * conv_out
    outputs = jnp.einsum("ij,jp->ip", scores, weighted, precision=precise)
    outputs = outputs + jnp.exp(log_keep)[:, None] * jnp.einsum(
        "in,pn->ip", c_rows, state_in, precision=precise
    )
    remains = jnp.exp(log_keep[-1] - log_keep)
    state_out = jnp.exp(log_keep[-1]) * state_in + jnp.einsum(
        "j,jp,jn->pn", remains, weighted, b_rows, precision=precise
    )
    return (outputs, state_out)


def strand_core(x_ext, gate_in, b_c, dt_raw, state_in, params):
    dt_bias_h, decay_rate, skip_h, conv_w = params
    conv_out = conv_silu(x_ext, conv_w)
    steps_dt = jax.nn.softplus(dt_raw + dt_bias_h)
    outputs, state_out = block_ssd(
        conv_out, steps_dt, b_c[:, :STATE], b_c[:, STATE:], decay_rate, state_in
    )
    gated = (outputs + skip_h * conv_out) * jax.nn.silu(gate_in)
    return (gated, state_out)


def strand_summary(x_ext, b_c, dt_raw, params):
    dt_bias_h, decay_rate, skip_h, conv_w = params
    conv_out = conv_silu(x_ext, conv_w)
    steps_dt = jax.nn.softplus(dt_raw + dt_bias_h)
    log_keep = jnp.cumsum(steps_dt * decay_rate)
    remains = jnp.exp(log_keep[-1] - log_keep) * steps_dt
    local_state = jnp.einsum("j,jp,jn->pn", remains, conv_out, b_c[:, :STATE], precision=precise)
    return (jnp.exp(log_keep[-1]), local_state)


def chain_step(earlier, following):
    return (earlier[0] * following[0], following[0] * earlier[1] + following[1])


def local(hidden, w_in, w_bc, w_dt, dt_bias, a_log, d_skip, conv_w, w_out, d_out):
    own_rows = hidden.shape[0]
    seq_rows = own_rows * lax.axis_size("tp")
    length_all = seq_rows * lax.axis_size("ctx")
    head_dim = w_out.shape[0]
    rim_rows = CONV - 1
    w_pair = jnp.concatenate([w_in, w_in[::-1]], axis=1)
    bc_pair = jnp.concatenate([w_bc, w_bc[::-1]], axis=1)
    dt_pair = jnp.concatenate([w_dt, w_dt[:, ::-1]], axis=0)
    out_pair = jnp.concatenate([w_out, w_out[:, ::-1]], axis=0)
    params = (dt_bias[0], -jnp.exp(a_log[0]), d_skip[0], conv_w)
    gathered = lax.all_gather(hidden, "tp", axis=0, tiled=True)
    projected = jnp.dot(gathered, w_pair, preferred_element_type=jnp.float32).astype(jnp.bfloat16)
    dt_raw = times_rows(gathered, dt_pair)
    b_c_all = jnp.dot(gathered, bc_pair, preferred_element_type=jnp.float32)
    x_both = jnp.concatenate(
        [projected[:, :head_dim], projected[:, 2 * head_dim : 3 * head_dim]], axis=1
    )
    x_halo = padded(x_both, (("ctx", 0),), rim_rows).astype(jnp.float32)
    x_ext = jnp.stack(
        [x_halo[: seq_rows + rim_rows, :head_dim], x_halo[rim_rows:, head_dim:][::-1]]
    )
    gate_in = jnp.stack(
        [projected[:, head_dim : 2 * head_dim], projected[::-1, 3 * head_dim :]]
    ).astype(jnp.float32)
    b_c = jnp.stack([b_c_all[:, : 2 * STATE], b_c_all[::-1, 2 * STATE :]])
    dt_both = jnp.stack([dt_raw[:, 0], dt_raw[::-1, 1]])
    decays, local_states = jax.vmap(strand_summary, in_axes=(0, 0, 0, None))(
        x_ext, b_c, dt_both, params
    )
    identity = (jnp.ones((), jnp.float32), jnp.zeros((head_dim, STATE), jnp.float32))
    fwd_in = entering((decays[0], local_states[0]), "ctx", chain_step, identity, False)[1]
    rev_in = entering((decays[1], local_states[1]), "ctx", chain_step, identity, True)[1]
    states_in = jnp.stack([fwd_in, rev_in])

    def core_both(x_part, gate_part, bc_part, dt_part, state_part):
        return jax.vmap(strand_core, in_axes=(0, 0, 0, 0, 0, None))(
            x_part, gate_part, bc_part, dt_part, state_part, params
        )

    (gated, states_out), pullback = jax.vjp(core_both, x_ext, gate_in, b_c, dt_both, states_in)
    gated_nat = jnp.concatenate([gated[0], gated[1][::-1]], axis=1).astype(jnp.bfloat16)
    portion = lax.all_gather(d_out, "tp", axis=0, tiled=True)
    grads_g = times_rows(portion, out_pair)
    grad_wout = across_rows(gated_nat, portion)
    grad_stack = jnp.stack([grads_g[:, :head_dim], grads_g[::-1, head_dim:]])
    direct = pullback((grad_stack, jnp.zeros_like(states_out)))
    direct_state = direct[4]
    fwd_adj = entering((decays[0], direct_state[0]), "ctx", chain_step, identity, True)[1]
    rev_adj = entering((decays[1], direct_state[1]), "ctx", chain_step, identity, False)[1]
    carried_grads = pullback((jnp.zeros_like(gated), jnp.stack([fwd_adj, rev_adj])))
    grad_x = direct[0] + carried_grads[0]
    grad_gates = direct[1] + carried_grads[1]
    grad_bcs = direct[2] + carried_grads[2]
    grad_dts = direct[3] + carried_grads[3]
    grad_x_rev = grad_x[1][::-1]
    grad_x_local = jnp.concatenate([grad_x[0][rim_rows:], grad_x_rev[:seq_rows]], axis=1)
    outgoing = jnp.concatenate([grad_x[0][:rim_rows], grad_x_rev[seq_rows:]], axis=0)
    incoming = padded(outgoing, (("ctx", 0),), rim_rows)
    grad_x_local = grad_x_local.at[:rim_rows, head_dim:].add(incoming[:rim_rows])
    grad_x_local = grad_x_local.at[seq_rows - rim_rows :, :head_dim].add(incoming[3 * rim_rows :])
    grad_proj = jnp.concatenate(
        [
            grad_x_local[:, :head_dim],
            grad_gates[0],
            grad_x_local[:, head_dim:],
            grad_gates[1][::-1],
        ],
        axis=1,
    ).astype(jnp.bfloat16)
    grad_bc = jnp.concatenate([grad_bcs[0], grad_bcs[1][::-1]], axis=1).astype(jnp.bfloat16)
    grad_dt = jnp.stack([grad_dts[0], grad_dts[1][::-1]], axis=1).astype(jnp.bfloat16)

    def strand_term(which):
        proj_cols = grad_proj[:, which * 2 * head_dim : (which + 1) * 2 * head_dim]
        wide_cols = w_pair[:, which * 2 * head_dim : (which + 1) * 2 * head_dim]
        bc_cols = grad_bc[:, which * 2 * STATE : (which + 1) * 2 * STATE]
        shared_cols = bc_pair[:, which * 2 * STATE : (which + 1) * 2 * STATE]
        dt_cols = grad_dt[:, which : which + 1]
        dt_rows = dt_pair[which : which + 1]
        summed = times_rows(proj_cols, wide_cols) + times_rows(bc_cols, shared_cols)
        return summed + jnp.dot(dt_cols, dt_rows, preferred_element_type=jnp.float32)

    forward_part = lax.psum_scatter(strand_term(0), "tp", scatter_dimension=0, tiled=True)
    reverse_part = lax.psum_scatter(strand_term(1), "tp", scatter_dimension=0, tiled=True)
    d_hidden = (forward_part + reverse_part).astype(jnp.bfloat16)
    scaling = 1.0 / math.sqrt(length_all)
    grad_pair = across_rows(gathered, grad_proj)
    d_w_in = (grad_pair[:, : 2 * head_dim] + grad_pair[::-1, 2 * head_dim :]) * scaling
    d_w_out = (grad_wout[:head_dim] + grad_wout[head_dim:, ::-1]) * scaling
    d_w_in, d_w_out = (
        lax.psum(d_w_in.astype(jnp.bfloat16), "ctx").astype(jnp.float32),
        lax.psum(d_w_out.astype(jnp.bfloat16), "ctx").astype(jnp.float32),
    )
    grad_bpair = across_rows(gathered, grad_bc)
    d_w_bc = lax.psum(
        (grad_bpair[:, : 2 * STATE] + grad_bpair[::-1, 2 * STATE :]) * scaling, ("ctx", "tp")
    )
    return (d_hidden, d_w_in, d_w_out, d_w_bc)


def solution(mesh):
    in_specs = (
        P(("ctx", "tp"), None),
        P(None, "tp"),
        P(),
        P("tp", None),
        P("tp"),
        P("tp"),
        P("tp"),
        P(None, "tp"),
        P("tp", None),
        P(("ctx", "tp"), None),
    )
    out_specs = (P(("ctx", "tp"), None), P(None, "tp"), P("tp", None), P())
    return jax.shard_map(local, mesh=mesh, in_specs=in_specs, out_specs=out_specs, check_vma=False)
```

profile of v0, /device:TPU:1, one launch (start us, length us, event | category | flops | bytes accessed | tf_op | source)
XLA Modules:
  0.0 1343.0 jit_solution(9077498691237861709)
XLA Ops:
  8.7 6.0 rev.53
  14.8 1.3 convert.70
  18.7 1.3 and_reduce_fusion
  20.6 1.4 slice_bitcast_fusion.12
  22.6 6.3 rev.55
  29.0 8.4 rev.49
  37.4 6.3 rev.51
  43.7 1.3 dynamic-slice.21
  45.7 1.3 dynamic-slice.19
  47.0 88.3 %all-gather.7.cloned.1.call-done = bf16[64,4,2048]{2,1,0:T(4,128)(2,1)} async-done(((bf16[1,4,2048]{2,1,0:T(4,128)(2,1)}), bf16[64,4,2048]{2,1,0:T(4,128)(2,1)}) %all-gather.7.cloned.1.call-update) | async-done | bytes 1048592 | tf_op jit(solution)/shard_map/all_gather | solution.py:122
  135.3 1.3 reshape.271
  142.1 2.1 slice_dynamic-update-slice_fusion
  144.9 107.4 %all-gather.5.cloned.1.call-done = bf16[64,4,2048]{2,1,0:T(4,128)(2,1)} async-done(((bf16[1,4,2048]{2,1,0:T(4,128)(2,1)}), bf16[64,4,2048]{2,1,0:T(4,128)(2,1)}) %all-gather.5.cloned.1.call-update) | async-done | bytes 1048592 | tf_op jit(solution)/shard_map/all_gather | solution.py:153
  252.3 1.3 reshape.269
  253.7 1.5 convolution_bitcast_fusion.2
  256.3 8.1 collective-permute-start
  267.4 62.4 %all_gather.29 = f32[8,64,16]{1,2,0:T(8,128)S(1)} all-gather(f32[1,64,16]{1,2,0:T(8,128)S(1)} %get-tuple-element.678), channel_id=1, replica_groups=mesh['ctx'=8,'tp'=64] {'ctx'}, dimensions={0}, use_global_device_ids=true | all-gather | bytes 36864 | tf_op jit(solution)/shard_map/all_gather | solution.py:30
  329.8 37.5 %all-reduce.19 = (f32[8]{0:T(128)S(1)}, f32[8]{0:T(128)S(1)}) all-reduce(f32[8]{0:T(128)} %slice_dynamic-update-slice_fusion, f32[8]{0:T(128)} %copy-done.65), channel_id=1, replica_groups=mesh['ctx'=8,'tp'=64] {'ctx'}, use_global_device_ids=true, to_apply=%add.17 | all-reduce | flops 16 | bytes 128
  367.3 10.2 while.62
  377.5 56.9 %all_gather.31 = f32[8,64,16]{1,2,0:T(8,128)S(1)} all-gather(f32[1,64,16]{1,2,0:T(8,128)S(1)} %get-tuple-element.679), channel_id=1, replica_groups=mesh['ctx'=8,'tp'=64] {'ctx'}, dimensions={0}, use_global_device_ids=true | all-gather | bytes 36864 | tf_op jit(solution)/shard_map/all_gather | solution.py:30
  434.4 10.1 while.63
  447.9 56.7 %all_gather.32 = f32[8,64,16]{1,2,0:T(8,128)S(1)} all-gather(f32[1,64,16]{1,2,0:T(8,128)S(1)} %get-tuple-element.676), channel_id=1, replica_groups=mesh['ctx'=8,'tp'=64] {'ctx'}, dimensions={0}, use_global_device_ids=true | all-gather | bytes 36864 | tf_op jit(solution)/shard_map/all_gather | solution.py:30
  504.7 10.1 while.64
  514.8 57.2 %all_gather.33 = f32[8,64,16]{1,2,0:T(8,128)S(1)} all-gather(f32[1,64,16]{1,2,0:T(8,128)S(1)} %get-tuple-element.677), channel_id=1, replica_groups=mesh['ctx'=8,'tp'=64] {'ctx'}, dimensions={0}, use_global_device_ids=true | all-gather | bytes 36864 | tf_op jit(solution)/shard_map/all_gather | solution.py:30
  572.0 10.2 while.65
  583.4 1.3 fusion.101
  584.7 1.3 fusion.92
  586.1 1.3 fusion.23
  588.6 1.6 fusion.127
  590.2 1.3 fusion.26
  592.2 1.4 multiply_reduce_fusion.3
  596.1 1.3 copy.38
  598.9 1.4 convolution_add_fusion.8
  601.4 2.1 fusion.188
  605.0 2.5 reduce-window.24
  608.5 2.5 reduce-window.26
  616.9 2.5 collective-permute-start.2
  619.4 1.5 collective-permute-start.3
  622.8 1.9 add_select_fusion
  624.7 2.0 scatter-add.6
  626.7 6.3 collective-permute-done.3
  636.5 7.5 rev.61
  647.1 1.7 fusion.31
  651.1 502.8 %all-reduce.28 = bf16[256,2048]{1,0:T(8,128)(2,1)S(1)} all-reduce(f32[256,2048]{1,0:T(8,128)S(1)} %fusion.6), channel_id=3, replica_groups=mesh['ctx'=8,'tp'=64] {'tp'}, use_global_device_ids=true, to_apply=%region_27.28.clone | all-reduce | flops 524288 | bytes 3145728
  1154.6 2.2 copy.41
  1156.8 1.8 convert_element_type.39
  1158.6 176.2 %all-reduce.25.cloned.1.call-done = f32[2048,32]{0,1:T(8,128)} async-done(((f32[2048,32]{0,1:T(8,128)}), f32[2048,32]{0,1:T(8,128)}) %all-reduce.25.cloned.1.call-update) | async-done | bytes 262160 | tf_op jit(solution)/shard_map/psum | solution.py:206
  1334.8 1.7 copy.111
  (321 shorter events, 83.7 us)
Async XLA Ops:
  7.2 129.5 %copy-start.27 = (bf16[1,2048]{1,0:T(2,128)(2,1)S(1)}, bf16[1,2048]{1,0:T(2,128)(2,1)}, u32[]{:S(2)}) copy-start(bf16[1,2048]{1,0:T(2,128)(2,1)} %param.25) | copy-start | bytes 12292
  7.2 128.1 %all-gather.7.cloned.1.call-start = ((), (), s32[]{:S(2)}) async-start(), calls=%async_computation.2 | async-start | bytes 1064960 | tf_op jit(solution)/shard_map/all_gather | solution.py:122
  7.9 244.4 %all-gather.5.cloned.1.call-start = ((), (), s32[]{:S(2)}) async-start(), calls=%async_computation.1 | async-start | bytes 1064960 | tf_op jit(solution)/shard_map/all_gather | solution.py:153
  8.7 1145.9 %all-reduce.27.cloned.1.call-start = ((), (), s32[]{:S(2)}) async-start(), calls=%async_computation.3 | async-start | bytes 1572864 | tf_op jit(solution)/shard_map/psum | solution.py:202
  29.0 109.9 %copy-start.5 = (bf16[2048,32]{0,1:T(8,128)(2,1)}, bf16[2048,32]{0,1:T(8,128)(2,1)S(1)}, u32[]{:S(2)}) copy-start(bf16[2048,32]{0,1:T(8,128)(2,1)S(1)} %rev.55) | copy-start | bytes 393220
  37.4 101.5 %copy-start.4 = (bf16[2048,32]{0,1:T(8,128)(2,1)S(1)}, bf16[2048,32]{0,1:T(8,128)(2,1)}, u32[]{:S(2)}) copy-start(bf16[2048,32]{0,1:T(8,128)(2,1)} %param.24) | copy-start | bytes 393220
  43.7 211.7 %copy-start.2 = (bf16[2048,128]{1,0:T(8,128)(2,1)}, bf16[2048,128]{1,0:T(8,128)(2,1)S(1)}, u32[]{:S(2)}) copy-start(bf16[2048,128]{1,0:T(8,128)(2,1)S(1)} %rev.51) | copy-start | bytes 1572868
  137.8 309.5 %copy-start.33 = (f32[256,1]{0,1:T(1,128)}, f32[256,1]{0,1:T(1,128)S(1)}, u32[]{:S(2)}) copy-start(f32[256,1]{0,1:T(1,128)S(1)} %rev.54) | copy-start | bytes 3076
  138.9 116.3 %copy-start.48 = (f32[1,2,2,128]{3,1,2,0:T(2,128)}, f32[1,2,2,128]{3,1,2,0:T(2,128)S(1)}, u32[]{:S(2)}) copy-start(f32[1,2,2,128]{3,1,2,0:T(2,128)S(1)} %copy.67) | copy-start | bytes 6148
  140.9 114.3 %copy-start.63 = (f32[2]{0:T(128)}, f32[2]{0:T(128)S(1)}, u32[]{:S(2)}) copy-start(f32[2]{0:T(128)S(1)} %slice_reduce_fusion.3) | copy-start | bytes 28
  144.9 110.3 %copy-start.65 = (f32[8]{0:T(128)}, f32[8]{0:T(128)S(1)}, u32[]{:S(2)}) copy-start(f32[8]{0:T(128)S(1)} %slice_dynamic-update-slice_fusion.1) | copy-start | bytes 100
  144.9 110.5 %copy-start = (bf16[2048,128]{1,0:T(8,128)(2,1)S(1)}, bf16[2048,128]{1,0:T(8,128)(2,1)}, u32[]{:S(2)}) copy-start(bf16[2048,128]{1,0:T(8,128)(2,1)} %param.23) | copy-start | bytes 1572868
  255.2 11.3 copy-start.15
  255.4 12.0 copy-start.14
  255.4 189.1 %copy-start.34 = (f32[1,256]{1,0:T(1,128)S(1)}, f32[1,256]{1,0:T(1,128)}, u32[]{:S(2)}) copy-start(f32[1,256]{1,0:T(1,128)} %get-tuple-element.686) | copy-start | bytes 3076
  255.9 189.2 %copy-start.42 = (f32[64]{0:T(128)S(1)}, f32[64]{0:T(128)}, u32[]{:S(2)}) copy-start(f32[64]{0:T(128)} %get-tuple-element.689) | copy-start | bytes 772
  255.9 189.2 %copy-start.44 = (f32[64]{0:T(128)S(1)}, f32[64]{0:T(128)}, u32[]{:S(2)}) copy-start(f32[64]{0:T(128)} %get-tuple-element.690) | copy-start | bytes 772
  256.0 189.2 %copy-start.46 = (f32[64]{0:T(128)S(1)}, f32[64]{0:T(128)}, u32[]{:S(2)}) copy-start(f32[64]{0:T(128)} %get-tuple-element.691) | copy-start | bytes 772
  256.0 189.2 %copy-start.53 = (f32[64]{0:T(128)S(1)}, f32[64]{0:T(128)}, u32[]{:S(2)}) copy-start(f32[64]{0:T(128)} %get-tuple-element.688) | copy-start | bytes 772
  256.0 189.7 %copy-start.21 = (f32[256,32]{0,1:T(8,128)S(1)}, f32[256,32]{0,1:T(8,128)}, u32[]{:S(2)}) copy-start(f32[256,32]{0,1:T(8,128)} %rev.56) | copy-start | bytes 98308
  256.0 189.7 %copy-start.23 = (f32[1,256,32]{1,2,0:T(8,128)S(1)}, f32[1,256,32]{1,2,0:T(8,128)}, u32[]{:S(2)}) copy-start(f32[1,256,32]{1,2,0:T(8,128)} %get-tuple-element.672) | copy-start | bytes 98308
  256.0 188.5 %copy-start.24 = (bf16[1,256,64]{1,2,0:T(8,128)(2,1)}, bf16[1,256,64]{1,2,0:T(8,128)(2,1)S(1)}, u32[]{:S(2)}) copy-start(bf16[1,256,64]{1,2,0:T(8,128)(2,1)S(1)} %get-tuple-element.658) | copy-start | bytes 98308
  256.2 188.4 %copy-start.18 = (bf16[256,64]{0,1:T(8,128)(2,1)}, bf16[256,64]{0,1:T(8,128)(2,1)S(1)}, u32[]{:S(2)}) copy-start(bf16[256,64]{0,1:T(8,128)(2,1)S(1)} %rev.52) | copy-start | bytes 98308
  256.3 188.2 %collective-permute-start = (bf16[3,128]{0,1:T(8,128)(2,1)S(1)}, bf16[3,128]{0,1:T(8,128)(2,1)S(1)}, u32[]{:S(2)}, u32[]{:S(2)}) collective-permute-start(bf16[3,128]{0,1:T(8,128)(2,1)S(1)} %get-tuple-element.670), channel_id=1, source_target_pairs={{0,64},{64,128},{128,192},{192,256},{256,320},{320,384},{384,448},... | collective-permute-start | bytes 2312 | tf_op jit(solution)/shard_map/ppermute | solution.py:22
  264.4 180.1 %collective-permute-start.1 = (bf16[3,128]{0,1:T(8,128)(2,1)S(1)}, bf16[3,128]{0,1:T(8,128)(2,1)S(1)}, u32[]{:S(2)}, u32[]{:S(2)}) collective-permute-start(bf16[3,128]{0,1:T(8,128)(2,1)S(1)} %get-tuple-element.671), channel_id=1, source_target_pairs={{64,0},{128,64},{192,128},{256,192},{320,256},{384,320},{448,384},... | collective-permute-start | bytes 2312 | tf_op jit(solution)/shard_map/ppermute | solution.py:23
  266.5 180.0 %copy-start.64 = (f32[2]{0:T(128)S(1)}, f32[2]{0:T(128)}, u32[]{:S(2)}) copy-start(f32[2]{0:T(128)} %copy-done.63) | copy-start | bytes 28
  266.5 180.8 %copy-start.35 = (f32[1,256]{1,0:T(1,128)S(1)}, f32[1,256]{1,0:T(1,128)}, u32[]{:S(2)}) copy-start(f32[1,256]{1,0:T(1,128)} %get-tuple-element.686) | copy-start | bytes 3076
  444.5 127.4 %copy-start.36 = (f32[2,256]{1,0:T(2,128)}, f32[2,256]{1,0:T(2,128)S(1)}, u32[]{:S(2)}) copy-start(f32[2,256]{1,0:T(2,128)S(1)} %compare_select_fusion.3) | copy-start | bytes 6148
  445.4 139.4 %copy-start.19 = (bf16[256,64]{0,1:T(8,128)(2,1)S(1)}, bf16[256,64]{0,1:T(8,128)(2,1)}, u32[]{:S(2)}) copy-start(bf16[256,64]{0,1:T(8,128)(2,1)} %copy-done.18) | copy-start | bytes 98308
  445.4 139.4 %copy-start.25 = (bf16[1,256,64]{1,2,0:T(8,128)(2,1)S(1)}, bf16[1,256,64]{1,2,0:T(8,128)(2,1)}, u32[]{:S(2)}) copy-start(bf16[1,256,64]{1,2,0:T(8,128)(2,1)} %copy-done.24) | copy-start | bytes 98308
  446.5 139.6 %copy-start.28 = (pred[256,256]{1,0:T(8,128)(4,1)S(1)}, pred[256,256]{1,0:T(8,128)(4,1)}, u32[]{:S(2)}) copy-start(pred[256,256]{1,0:T(8,128)(4,1)} %iota_compare_fusion) | copy-start | bytes 196612
  446.5 139.6 %copy-start.49 = (f32[1,2,2,128]{3,1,2,0:T(2,128)S(1)}, f32[1,2,2,128]{3,1,2,0:T(2,128)}, u32[]{:S(2)}) copy-start(f32[1,2,2,128]{3,1,2,0:T(2,128)} %copy-done.48) | copy-start | bytes 6148
  583.2 9.0 copy-start.22
  598.9 4.7 copy-start.55
  598.9 4.7 copy-start.56
  598.9 4.7 copy-start.57
  598.9 4.7 copy-start.58
  598.9 4.7 copy-start.59
  598.9 4.7 copy-start.60
  598.9 4.7 copy-start.61
  598.9 4.7 copy-start.62
  604.5 29.7 %copy-start.7 = (bf16[256,64]{0,1:T(8,128)(2,1)}, bf16[256,64]{0,1:T(8,128)(2,1)S(1)}, u32[]{:S(2)}) copy-start(bf16[256,64]{0,1:T(8,128)(2,1)S(1)} %rev.58) | copy-start | bytes 98308
  604.8 16.8 %copy-start.16 = (bf16[256,32]{0,1:T(8,128)(2,1)}, bf16[256,32]{0,1:T(8,128)(2,1)S(1)}, u32[]{:S(2)}) copy-start(bf16[256,32]{0,1:T(8,128)(2,1)S(1)} %get-tuple-element.674) | copy-start | bytes 49156
  613.7 7.3 copy-start.51
  613.7 7.3 copy-start.52
  616.9 5.8 collective-permute-start.2
  619.4 13.6 %collective-permute-start.3 = (f32[3,64]{0,1:T(8,128)}, f32[3,64]{0,1:T(8,128)S(1)}, u32[]{:S(2)}, u32[]{:S(2)}) collective-permute-start(f32[3,64]{0,1:T(8,128)} %get-tuple-element.638), channel_id=1, source_target_pairs={{64,0},{128,64},{192,128},{256,192},{320,256},{384,320},{448,384},... | collective-permute-start | bytes 2312 | tf_op jit(solution)/shard_map/ppermute | solution.py:23
  645.0 689.8 %all-reduce.25.cloned.1.call-start = ((), (), s32[]{:S(2)}) async-start(), calls=%async_computation | async-start | bytes 524288 | tf_op jit(solution)/shard_map/psum | solution.py:206
  (29 other events, 83.4 us)
Sparse Core Ops, SparseCore 0:
  10.2 125.1 all-gather.6
  137.5 114.7 all-gather.4
  645.1 228.5 all-reduce.26
  879.9 454.8 all-reduce.24
where the time goes:
time: 1350 us; the launch traced here: 1340 us
  blocking collectives  773 us (57%)
  waiting for transfers between devices  380 us (28%)
  local copies, waits for them, and re-layouts  87.5 us (6%)
  other arithmetic  44.4 us (3%)
  matrix products  25.8 us (2%)
  between operations  17.6 us (1%)
  starting transfers between devices  13.6 us (1%)
    unnamed x2, blocking collectives  540 us
    all_gather x4, blocking collectives, entering(): everything = jax.tree.map(lambda part: lax.all_gather(part, axis), array)  233 us
    psum x1, waiting for transfers between devices, local(): lax.psum((grad_bpair[:, :2 * STATE] + grad_bpair[::-1, 2 * STATE:]) * sca...  176 us
    all_gather x1, waiting for transfers between devices, local(): portion = lax.all_gather(d_out, 'tp', axis=0, tiled=True)  107 us
    all_gather x1, waiting for transfers between devices, local(): gathered = lax.all_gather(hidden, 'tp', axis=0, tiled=True)  88.3 us
  transfers between devices with their start and end apart: 8, of which 4 were waited for; matrix products, arithmetic and copies ran while one was open for 6% of the time, Pallas kernels for 0%

commit v1 on v0

v1 whole, which is shorter than its diff:
```python
import math

import jax
import jax.numpy as jnp
from jax import lax
from jax.experimental import pallas as pl
from jax.experimental.pallas import tpu as pltpu
from jax.sharding import PartitionSpec as P

MESH = pl.DeviceIdType.MESH
BF = jnp.bfloat16
F32 = jnp.float32


def place():
    ctx, tp = lax.axis_index("ctx"), lax.axis_index("tp")
    y, zh = ctx // 2, ctx % 2
    x, zl, core = tp // 16, (tp // 2) % 8, tp % 2
    return x, y, zh * 8 + zl, core


def dev(x, y, z, core):
    return (y * 2 + z // 8, x * 16 + (z % 8) * 2 + core)


def greet(peers):
    barrier = pltpu.get_barrier_semaphore()
    for peer in peers:
        pl.semaphore_signal(barrier, inc=1, device_id=peer, device_id_type=MESH)
    pl.semaphore_wait(barrier, len(peers))


def send(src, dst, ssem, rsem, peer):
    copy = pltpu.make_async_remote_copy(src_ref=src, dst_ref=dst, send_sem=ssem, recv_sem=rsem, device_id=peer, device_id_type=MESH)
    copy.start()
    return copy


def gather_kernel(h_ref, g_ref, own_ref, oth_ref, swap, asm, s_core, r_core, zs, zr, xs, xr, cs, cr, ys, yr):
    x, y, z, core = place()
    half = 1024
    right, left = lax.rem(x + 1, 4), lax.rem(x + 3, 4)
    up, down = lax.rem(z + 1, 16), lax.rem(z + 15, 16)
    north, south = lax.rem(y + 1, 4), lax.rem(y + 3, 4)
    other = dev(x, y, z, 1 - core)
    p_up, p_down = dev(x, y, up, core), dev(x, y, down, core)
    p_right, p_left = dev(right, y, z, core), dev(left, y, z, core)
    p_north, p_south = dev(x, north, z, core), dev(x, south, z, core)
    greet([other, p_up, p_down, p_right, p_left, p_north, p_south])

    def blk(xx, zz):
        return 1 + (zz // 8) * 32 + xx * 8 + zz % 8

    mine = pl.ds(pl.multiple_of(core * half, half), half)
    theirs = pl.ds(pl.multiple_of((1 - core) * half, half), half)
    a = send(h_ref.at[:, theirs], swap.at[0], s_core.at[0], r_core.at[0], other)
    b = send(g_ref.at[:, theirs], swap.at[1], s_core.at[1], r_core.at[1], other)
    own_blk = blk(x, z)
    a.wait()
    b.wait()
    for k, ref in ((0, h_ref), (1, g_ref)):
        local = ref[:, mine].astype(F32)
        remote = swap[k].astype(F32)
        first = jnp.where(core == 0, local, remote)
        second = jnp.where(core == 0, remote, local)
        asm[0:4, :] = first
        asm[4:8, :] = second
        own_ref[k, own_blk] = asm[...].astype(BF)

    pend = []

    def cross(b, slot):
        pend.append(send(own_ref.at[:, b], oth_ref.at[:, b], cs.at[slot], cr.at[slot], other))

    def spread(zz, b, slot):
        pend.append(send(own_ref.at[:, b], own_ref.at[:, b], xs.at[0, slot], xr.at[0, slot], p_right))
        pend.append(send(own_ref.at[:, b], own_ref.at[:, b], xs.at[1, slot], xr.at[1, slot], p_left))
        cross(b, slot)

    def landed(b, sem, peer):
        pltpu.make_async_remote_copy(src_ref=own_ref.at[:, b], dst_ref=own_ref.at[:, b], send_sem=cs.at[0], recv_sem=sem, device_id=peer, device_id_type=MESH).wait_recv()

    def x_arrivals(zz, slot, forward_right):
        bl, br = blk(left, zz), blk(right, zz)
        landed(bl, xr.at[0, slot], p_left)
        if forward_right:
            pend.append(send(own_ref.at[:, bl], own_ref.at[:, bl], xs.at[2, slot], xr.at[2, slot], p_right))
        cross(bl, 16 + slot)
        landed(br, xr.at[1, slot], p_right)
        if not forward_right:
            pend.append(send(own_ref.at[:, br], own_ref.at[:, br], xs.at[2, slot], xr.at[2, slot], p_left))
        cross(br, 32 + slot)

    def far_arrival(zz, slot, forward_right):
        bo = blk(lax.rem(x + 2, 4), zz)
        landed(bo, xr.at[2, slot], p_left if forward_right else p_right)
        cross(bo, 48 + slot)

    pend.append(send(own_ref.at[:, own_blk], own_ref.at[:, own_blk], zs.at[0, 0], zr.at[0, 0], p_up))
    pend.append(send(own_ref.at[:, own_blk], own_ref.at[:, own_blk], zs.at[1, 0], zr.at[1, 0], p_down))
    spread(z, own_blk, 0)
    levels = [[(z, 0)]]
    for s in range(1, 9):
        level = []
        zz = lax.rem(z + 16 - s, 16)
        b = blk(x, zz)
        landed(b, zr.at[0, s - 1], p_down)
        if s < 8:
            pend.append(send(own_ref.at[:, b], own_ref.at[:, b], zs.at[0, s], zr.at[0, s], p_up))
        spread(zz, b, s)
        level.append((zz, s))
        if s < 8:
            zz = lax.rem(z + s, 16)
            b = blk(x, zz)
            landed(b, zr.at[1, s - 1], p_up)
            if s < 7:
                pend.append(send(own_ref.at[:, b], own_ref.at[:, b], zs.at[1, s], zr.at[1, s], p_down))
            spread(zz, b, 8 + s)
            level.append((zz, 8 + s))
        levels.append(level)
        for zz, slot in levels[s - 1]:
            x_arrivals(zz, slot, slot % 2 == 0)
        if s >= 2:
            for zz, slot in levels[s - 2]:
                far_arrival(zz, slot, slot % 2 == 0)
    for zz, slot in levels[8]:
        x_arrivals(zz, slot, slot % 2 == 0)
    for s in (7, 8):
        for zz, slot in levels[s]:
            far_arrival(zz, slot, slot % 2 == 0)
    pend.append(send(own_ref.at[:, 64], own_ref.at[:, 0], ys.at[0], yr.at[0], p_north))
    pend.append(send(own_ref.at[:, 1], own_ref.at[:, 65], ys.at[1], yr.at[1], p_south))
    landed(0, yr.at[0], p_south)
    cross(0, 64)
    landed(65, yr.at[1], p_north)
    cross(65, 65)
    for slot in range(66):
        pltpu.make_async_remote_copy(src_ref=own_ref.at[:, 0], dst_ref=oth_ref.at[:, 0], send_sem=cs.at[0], recv_sem=cr.at[slot], device_id=other, device_id_type=MESH).wait_recv()
    for copy in pend:
        copy.wait_send()


def gather(h, g):
    out = jax.ShapeDtypeStruct((2, 66, 8, 1024), BF)
    D = pltpu.SemaphoreType.DMA
    return pl.pallas_call(
        gather_kernel,
        out_shape=(out, out),
        in_specs=[pl.BlockSpec(memory_space=pltpu.VMEM)] * 2,
        out_specs=[pl.BlockSpec(memory_space=pltpu.VMEM)] * 2,
        scratch_shapes=[
            pltpu.VMEM((2, 4, 1024), BF), pltpu.VMEM((8, 1024), F32),
            D((2,)), D((2,)), D((2, 8)), D((2, 8)), D((3, 16)), D((3, 16)), D((66,)), D((66,)), D((2,)), D((2,)),
        ],
        compiler_params=pltpu.CompilerParams(collective_id=0, has_side_effects=True, vmem_limit_bytes=40 << 20),
        name="gather_rows",
    )(h, g)

BF, F32 = jnp.bfloat16, jnp.float32
ROWS, EXT, D, HALF, CH = 512, 528, 2048, 1024, 256


def mm(a, b, dims):
    return lax.dot_general(a, b, (dims, ((), ())), preferred_element_type=F32)


def nn(a, b):
    return mm(a, b, ((1,), (0,)))


def nt(a, b):
    return mm(a, b, ((1,), (1,)))


def tn(a, b):
    return mm(a, b, ((0,), (0,)))


def iota(shape, dim):
    return lax.broadcasted_iota(jnp.int32, shape, dim)


def flipper():
    return (iota((256, 256), 0) + iota((256, 256), 1) == 255).astype(F32).astype(BF)


def tri(lower):
    a, b = iota((CH, CH), 0), iota((CH, CH), 1)
    return ((a >= b) if lower else (a <= b)).astype(F32).astype(BF)


def split3(v):
    h = v.astype(BF)
    m = (v - h.astype(F32)).astype(BF)
    l = (v - h.astype(F32) - m.astype(F32)).astype(BF)
    return h, m, l


def exact_left(t, v):
    h, m, l = split3(v)
    return (nn(t, l) + nn(t, m)) + nn(t, h)


def exact_right(v, t):
    h, m, l = split3(v)
    return (nn(l, t) + nn(m, t)) + nn(h, t)


def fwd_lanes(shape):
    return iota(shape, 1) < 64


def prepare_kernel(at_ref, par_ref, own_ref, oth_ref, wcat_ref, wout_ref, w7_ref,
                   wf_ref, pre_ref, z_ref, dtr_ref, gg_ref, bc_ref, cum_ref, sums_ref, total_ref, x_scr, wo_scr):
    y, core = at_ref[0], at_ref[1]
    bias, rate = par_ref[0], par_ref[1]
    flip = flipper()
    for q in range(8):
        wf_ref[q * 256:(q + 1) * 256, :] = nn(flip, wcat_ref[(7 - q) * 256:(8 - q) * 256, :]).astype(BF)
        wo_scr[0:64, q * 256:(q + 1) * 256] = wout_ref[:, q * 256:(q + 1) * 256]
        wo_scr[64:128, q * 256:(q + 1) * 256] = nn(wout_ref[:, (7 - q) * 256:(8 - q) * 256], flip).astype(BF)
    mine = pl.ds(pl.multiple_of(core * HALF, HALF), HALF)
    theirs = pl.ds(pl.multiple_of((1 - core) * HALF, HALF), HALF)
    h_own, h_oth = own_ref[0:EXT, :], oth_ref[0:EXT, :]
    pf = nn(h_own, wcat_ref[mine, :]) + nn(h_oth, wcat_ref[theirs, :])
    pr = nn(h_own, wf_ref[mine, :]) + nn(h_oth, wf_ref[theirs, :])
    g_own, g_oth = own_ref[EXT:2 * EXT, :], oth_ref[EXT:2 * EXT, :]
    gg = nt(g_own, wo_scr[:, mine]) + nt(g_oth, wo_scr[:, theirs])
    gg = gg[8:8 + ROWS]
    gg_ref[...] = gg
    first = pltpu.roll(pr[:, 0:128], 64, 1)
    lanes = fwd_lanes((EXT, 128))
    x2 = jnp.where(lanes, pf[:, 0:128], first).astype(BF).astype(F32)
    z2 = jnp.where(lanes, pltpu.roll(pf[:, 0:128], 64, 1), pr[:, 0:128]).astype(BF).astype(F32)
    row = iota((EXT, 128), 0)
    outside = ((row < 8) & (y == 0)) | ((row >= 8 + ROWS) & (y == 3))
    x_scr[...] = jnp.where(outside, 0.0, x2)
    pre = w7_ref[0:1, :] * x_scr[5:5 + ROWS, :]
    for k in range(1, 7):
        pre = pre + w7_ref[k:k + 1, :] * x_scr[5 + k:5 + k + ROWS, :]
    pre_ref[...] = pre
    z2 = z2[8:8 + ROWS]
    z_ref[...] = z2
    bf, br = pf[8:8 + ROWS, 128:256], pr[8:8 + ROWS, 128:256]
    bc_ref[0] = bf.astype(BF)
    bc_ref[1] = br.astype(BF)
    lanes = fwd_lanes((ROWS, 128))
    dtr = jnp.where(lanes, bf[:, 32:33], br[:, 32:33]) + bias
    dtr_ref[...] = dtr
    dt = jnp.maximum(dtr, 0.0) + jnp.log1p(jnp.exp(-jnp.abs(dtr)))
    xc = pre * jax.nn.sigmoid(pre)
    u = dt * xc
    dy = gg * (z2 * jax.nn.sigmoid(z2))
    la = dt * rate
    low, upp = tri(True), tri(False)
    lanes = fwd_lanes((CH, 128))
    lane1, lane16 = fwd_lanes((1, 128)), fwd_lanes((16, 128))
    ends, sts, ads = [], [], []
    for c in range(2):
        rows = slice(c * CH, (c + 1) * CH)
        cum = jnp.where(lanes, exact_left(low, la[rows]), exact_left(upp, la[rows]))
        cum_ref[rows, :] = cum
        end = jnp.where(lane1, cum[CH - 1:CH], cum[0:1])
        ru = (jnp.exp(end - cum) * u[rows]).astype(BF)
        ed = (jnp.exp(cum) * dy[rows]).astype(BF)
        b0, b1 = bf[rows].astype(BF), br[rows].astype(BF)
        st = jnp.where(lane16, tn(b0, ru)[0:16], tn(b1, ru)[0:16])
        ad = jnp.where(lane16, tn(b0, ed)[16:32], tn(b1, ed)[16:32])
        sums_ref[c, 0:16, :] = st
        sums_ref[c, 16:32, :] = ad
        ends.append(end)
        sts.append(st)
        ads.append(ad)
    e0, e1 = jnp.exp(ends[0]), jnp.exp(ends[1])
    total_ref[0:16, :] = jnp.where(lane16, e1 * sts[0] + sts[1], e0 * sts[1] + sts[0])
    total_ref[16:32, :] = jnp.where(lane16, ads[0] + e0 * ads[1], ads[1] + e1 * ads[0])
    total_ref[32:40, :] = jnp.broadcast_to(jnp.exp(ends[0] + ends[1]), (8, 128))


def scan_kernel(at_ref, par_ref, all_ref, pre_ref, z_ref, dtr_ref, gg_ref, bc_ref, cum_ref, sums_ref,
                gated_ref, dpre_ref, dz_ref, tail_ref):
    y = at_ref[0]
    rate, skip = par_ref[1], par_ref[2]
    lane16, lane1 = fwd_lanes((16, 128)), fwd_lanes((1, 128))
    s_f = jnp.zeros((16, 128), F32)
    s_r, e_f, e_r = s_f, s_f, s_f
    for k in range(4):
        st, ad, dk = all_ref[k, 0:16, :], all_ref[k, 16:32, :], all_ref[k, 32:33, :]
        s_f = jnp.where(k < y, dk * s_f + st, s_f)
        e_r = jnp.where(k < y, dk * e_r + ad, e_r)
    for k in (3, 2, 1, 0):
        st, ad, dk = all_ref[k, 0:16, :], all_ref[k, 16:32, :], all_ref[k, 32:33, :]
        s_r = jnp.where(k > y, dk * s_r + st, s_r)
        e_f = jnp.where(k > y, dk * e_f + ad, e_f)
    state, adj = jnp.where(lane16, s_f, s_r), jnp.where(lane16, e_f, e_r)
    ends = []
    for c in range(2):
        cum = cum_ref[c * CH:(c + 1) * CH, :]
        ends.append(jnp.exp(jnp.where(lane1, cum[CH - 1:CH], cum[0:1])))
    st0, st1 = sums_ref[0, 0:16, :], sums_ref[1, 0:16, :]
    ad0, ad1 = sums_ref[0, 16:32, :], sums_ref[1, 16:32, :]
    s_in = [jnp.where(lane16, state, ends[1] * state + st1), jnp.where(lane16, ends[0] * state + st0, state)]
    e_out = [jnp.where(lane16, ad1 + ends[1] * adj, adj), jnp.where(lane16, adj, ad0 + ends[0] * adj)]
    s_out = [ends[0] * s_in[0] + st0, ends[1] * s_in[1] + st1]
    lanes = fwd_lanes((CH, 128))
    low, upp = tri(True), tri(False)
    same = ((iota((128, 128), 0) < 64) == (iota((128, 128), 1) < 64)).astype(F32).astype(BF)
    ii, jj = iota((CH, CH), 0), iota((CH, CH), 1)
    for c in range(2):
        rows = slice(c * CH, (c + 1) * CH)
        pre, z, dtr, gg, cum = (r[rows, :] for r in (pre_ref, z_ref, dtr_ref, gg_ref, cum_ref))
        sg, sz = jax.nn.sigmoid(pre), jax.nn.sigmoid(z)
        xc, gate = pre * sg, z * sz
        dt = jnp.maximum(dtr, 0.0) + jnp.log1p(jnp.exp(-jnp.abs(dtr)))
        u, dy = dt * xc, gg * gate
        ub, dyb = u.astype(BF), dy.astype(BF)
        end = jnp.where(lane1, cum[CH - 1:CH], cum[0:1])
        rem, grow = jnp.exp(end - cum), jnp.exp(cum)
        cum_t = cum.T
        sb, eb = s_in[c].astype(BF), e_out[c].astype(BF)
        zero = jnp.zeros_like(dyb)
        y_s, du_s, tails = [], [], []
        for s in range(2):
            bc = bc_ref[s, rows, :]
            b, cc = bc[:, 0:16], bc[:, 16:32]
            col, line = cum[:, 64 * s:64 * s + 1], cum_t[64 * s:64 * s + 1, :]
            mask = (ii >= jj) if s == 0 else (ii <= jj)
            decay = jnp.exp(jnp.where(mask, col - line, -1e30))
            w = (nt(cc, b) * decay).astype(BF)
            rem_c, grow_c = rem[:, 64 * s:64 * s + 1], grow[:, 64 * s:64 * s + 1]
            y_s.append(nn(w, ub) + grow_c * nn(cc, sb))
            du_s.append(tn(w, dyb) + rem_c * nn(b, eb))
            dym = jnp.where(lanes if s == 0 else ~lanes, dy, 0.0).astype(BF)
            um = jnp.where(lanes if s == 0 else ~lanes, u, 0.0).astype(BF)
            ds = (nt(dym, ub) * decay).astype(BF)
            dc = nn(ds, b) + grow_c * nt(dym, sb)
            db = tn(ds, cc) + rem_c * nt(um, eb)
            tails.append((db, dc))
        y2, du = jnp.where(lanes, y_s[0], y_s[1]), jnp.where(lanes, du_s[0], du_s[1])
        inner = dyb.astype(F32) * y2 - ub.astype(F32) * du
        dl = exact_right(inner, same)
        direct = exact_right(du * xc, same)
        const = jnp.sum(e_out[c] * s_out[c], axis=0, keepdims=True)
        const = exact_right(jnp.broadcast_to(const, (16, 128)), same)[0:1]
        dla = jnp.where(lanes, exact_left(upp, dl), exact_left(low, dl)) + const
        ddt = (rate * dla + direct) * jax.nn.sigmoid(dtr)
        dxc = du * dt + skip * dy
        full = y2 + skip * xc
        gated_ref[rows, :] = full * gate
        dz_ref[rows, :] = gg * full * (sz * (1.0 + z * (1.0 - sz)))
        dpre_ref[rows, :] = dxc * (sg * (1.0 + pre * (1.0 - sg)))
        for s in range(2):
            db, dc = tails[s]
            pad = jnp.zeros((CH, 95), F32)
            tail_ref[s, rows, :] = jnp.concatenate([db, dc, ddt[:, 64 * s:64 * s + 1], pad], axis=1)


def finish_kernel(at_ref, edge_ref, own_ref, oth_ref, wcat_ref, wf_ref, w7_ref, gated_ref, dpre_ref, dz_ref, tail_ref,
                  gin_ref, dw_ref, d_scr, ext_scr, gcat, acc):
    y, core, zh = at_ref[0], at_ref[1], at_ref[2]
    flip = flipper()
    scaling = 1.0 / math.sqrt(D)
    d_scr[8:8 + ROWS, :] = dpre_ref[...]
    d_scr[0:8, :] = jnp.where(y == 0, 0.0, edge_ref[0])
    d_scr[8 + ROWS:EXT, :] = jnp.where(y == 3, 0.0, edge_ref[1])
    dx = w7_ref[6:7, :] * d_scr[5:5 + ROWS, :]
    for k in range(1, 7):
        dx = dx + w7_ref[6 - k:7 - k, :] * d_scr[5 + k:5 + k + ROWS, :]
    dz = dz_ref[...]
    lanes = fwd_lanes((ROWS, 128))
    parts = (jnp.where(lanes, dx, pltpu.roll(dz, 64, 1)), jnp.where(lanes, pltpu.roll(dx, 64, 1), dz))
    ext_scr[0:8, :] = jnp.zeros((8, 640), F32)
    ext_scr[8 + ROWS:EXT, :] = jnp.zeros((8, 640), F32)
    for s in range(2):
        gcat[:, s * 256:s * 256 + 128] = parts[s].astype(BF)
        gcat[:, s * 256 + 128:s * 256 + 256] = tail_ref[s].astype(BF)
        ext_scr[8:8 + ROWS, s * 256:s * 256 + 128] = parts[s]
        ext_scr[8:8 + ROWS, s * 256 + 128:s * 256 + 256] = tail_ref[s]
    ext_scr[8:8 + ROWS, 512:640] = gated_ref[...]
    ext = ext_scr[...].astype(BF)
    mine = pl.ds(pl.multiple_of(core * HALF, HALF), HALF)
    theirs = pl.ds(pl.multiple_of((1 - core) * HALF, HALF), HALF)
    acc[0:512, mine] = tn(ext[:, 0:512], own_ref[0:EXT, :])
    acc[0:512, theirs] = tn(ext[:, 0:512], oth_ref[0:EXT, :])
    acc[512:640, mine] = tn(ext[:, 512:640], own_ref[EXT:2 * EXT, :])
    acc[512:640, theirs] = tn(ext[:, 512:640], oth_ref[EXT:2 * EXT, :])
    for q in range(8):
        cols, back = slice(q * 256, (q + 1) * 256), slice((7 - q) * 256, (8 - q) * 256)
        w = acc[0:160, cols] + nn(acc[256:416, back].astype(BF), flip)
        dw_ref[0:128, cols] = (w[0:128] * scaling).astype(BF)
        wb = (w[128:160] * scaling).astype(BF)
        half, m = q // 4, (q % 4) * 2
        gin_ref[half, m * 32:(m + 1) * 32, HALF:HALF + 128] = wb[:, 0:128]
        gin_ref[half, (m + 1) * 32:(m + 2) * 32, HALF:HALF + 128] = wb[:, 128:256]
        w = acc[512:576, cols] + nn(acc[576:640, back].astype(BF), flip)
        dw_ref[128:192, cols] = (w * scaling).astype(BF)
    local = pl.ds(pl.multiple_of(zh * 256, 256), 256)
    for k in range(2):
        g = nt(gcat[local, 0:256], wcat_ref[k * HALF:(k + 1) * HALF, :]) + nt(gcat[local, 256:512], wf_ref[k * HALF:(k + 1) * HALF, :])
        gin_ref[k, :, 0:HALF] = g.astype(BF)


V = pl.BlockSpec(memory_space=pltpu.VMEM)
S = pl.BlockSpec(memory_space=pltpu.SMEM)


def out(*shape, dtype=F32):
    return jax.ShapeDtypeStruct(shape, dtype)


def params():
    return pltpu.CompilerParams(vmem_limit_bytes=56 << 20)


def prepare(at, par, own, oth, wcat, wout, w7, **kw):
    return pl.pallas_call(
        prepare_kernel,
        out_shape=(out(D, 256, dtype=BF), out(ROWS, 128), out(ROWS, 128), out(ROWS, 128), out(ROWS, 128),
                   out(2, ROWS, 128, dtype=BF), out(ROWS, 128), out(2, 32, 128), out(40, 128)),
        in_specs=[S, S] + [V] * 5, out_specs=[V] * 9,
        scratch_shapes=[pltpu.VMEM((EXT, 128), F32), pltpu.VMEM((128, D), BF)],
        compiler_params=params(), name="prepare", **kw,
    )(at, par, own, oth, wcat, wout, w7)


def scan(at, par, everything, pre, z, dtr, gg, bc, cum, sums, **kw):
    return pl.pallas_call(
        scan_kernel,
        out_shape=(out(ROWS, 128), out(ROWS, 128), out(ROWS, 128), out(2, ROWS, 128)),
        in_specs=[S, S] + [V] * 8, out_specs=[V] * 4,
        compiler_params=params(), name="scan", **kw,
    )(at, par, everything, pre, z, dtr, gg, bc, cum, sums)


def finish(at, edge, own, oth, wcat, wf, w7, gated, dpre, dz, tail, **kw):
    return pl.pallas_call(
        finish_kernel,
        out_shape=(out(2, 256, HALF + 128, dtype=BF), out(192, D, dtype=BF)),
        in_specs=[S] + [V] * 10, out_specs=[V] * 2,
        scratch_shapes=[pltpu.VMEM((EXT, 128), F32), pltpu.VMEM((EXT, 640), F32), pltpu.VMEM((ROWS, 512), BF), pltpu.VMEM((640, D), F32)],
        compiler_params=params(), name="finish", **kw,
    )(at, edge, own, oth, wcat, wf, w7, gated, dpre, dz, tail)


def weights(w_in, w_bc, w_dt, conv_w):
    wcat = jnp.concatenate([w_in, w_bc, w_dt.T, jnp.zeros((D, 95), BF)], axis=1)
    gap = jnp.zeros((3, 64), F32)
    w7 = jnp.concatenate([jnp.concatenate([conv_w, gap], 0), jnp.concatenate([gap, conv_w[::-1]], 0)], axis=1)
    return wcat, jnp.concatenate([w7, jnp.zeros((1, 128), F32)], axis=0)

def ring_y(x, y, z, core):
    return [dev(x, lax.rem(y + k, 4), z, core) for k in (1, 2, 3)]


def states_kernel(total_ref, all_ref, ss, rs):
    x, y, z, core = place()
    peers = ring_y(x, y, z, core)
    greet(peers)
    all_ref[y] = total_ref[...]
    copies = [send(total_ref, all_ref.at[y], ss.at[k], rs.at[k], peers[k]) for k in range(3)]
    for k in range(3):
        copies[k].wait_send()
        came = lax.rem(y + 3 - k, 4)
        pltpu.make_async_remote_copy(src_ref=total_ref, dst_ref=all_ref.at[came], send_sem=ss.at[k], recv_sem=rs.at[k], device_id=peers[k], device_id_type=MESH).wait_recv()


def edges_kernel(dpre_ref, edge_ref, ss, rs):
    x, y, z, core = place()
    north, south = dev(x, lax.rem(y + 1, 4), z, core), dev(x, lax.rem(y + 3, 4), z, core)
    greet([north, south])
    a = send(dpre_ref.at[ROWS - 8:ROWS, :], edge_ref.at[0], ss.at[0], rs.at[0], north)
    b = send(dpre_ref.at[0:8, :], edge_ref.at[1], ss.at[1], rs.at[1], south)
    a.wait()
    b.wait()


def reduce_kernel(gin_ref, dw_ref, hid_ref, dwo_ref, fg_ref,
                  rc, w1, rx, w2, rz, hs, hr, fy, ry, e1, k1, e2,
                  cs, cr, xs, xr, zs, zr, ys, yr, fs, fr, es, er):
    x, y, z, core = place()
    zh, zl = z // 8, z % 8
    other = dev(x, y, z, 1 - core)
    xp = [dev(lax.rem(x + k, 4), y, z, core) for k in (1, 2, 3)]
    yp = ring_y(x, y, z, core)
    zp = [dev(x, y, zh * 8 + lax.rem(zl + k, 8), core) for k in range(1, 8)]
    greet([other] + xp + yp + zp)
    pend = []

    def go(src, dst, ssem, rsem, peer):
        copy = send(src, dst, ssem, rsem, peer)
        pend.append(copy)
        return copy

    near, far = dev(x, y + 1 - 2 * lax.rem(y, 2), z, core), dev(x, 3 - y, z, core)
    turn, side = lax.rem((y + 1) // 2, 2), y // 2
    plan = ((near, turn, far, side), (far, side, near, turn))

    def rows_of(k):
        return pl.ds(pl.multiple_of(k * 96, 96), 96)

    def cols_of(h, k):
        return pl.ds(pl.multiple_of(h * 1024 + k * 512, 512), 512)

    dc = go(gin_ref.at[1 - core], rc, cs.at[0], cr.at[0], other)
    s1 = []
    for h in range(2):
        p1, k1h, _, _ = plan[h]
        s1.append(go(dw_ref.at[rows_of(1 - k1h), h * 1024:(h + 1) * 1024], e1.at[h], es.at[h, 0], er.at[h, 0], p1))
    dc.wait_recv()
    for k in range(4):
        w1[k] = (gin_ref[core, k * 64:(k + 1) * 64, :].astype(F32) + rc[k * 64:(k + 1) * 64, :].astype(F32)).astype(BF)
    sx = [go(w1.at[lax.rem(x + k, 4)], rx.at[k - 1], xs.at[k - 1], xr.at[k - 1], xp[k - 1]) for k in (1, 2, 3)]
    s2 = []
    for h in range(2):
        _, k1h, p2, k2h = plan[h]
        s1[h].wait_recv()
        for q in range(2):
            c = slice(h * 1024 + q * 512, h * 1024 + (q + 1) * 512)
            k1[h, q] = (dw_ref[rows_of(k1h), c].astype(F32) + e1[h, :, q * 512:(q + 1) * 512].astype(F32)).astype(BF)
        s2.append(go(k1.at[h, 1 - k2h], e2.at[h], es.at[h, 1], er.at[h, 1], p2))
    for c in sx:
        c.wait_recv()
    for k in range(8):
        r = slice(k * 8, (k + 1) * 8)
        w2[k] = (w1[x, r, :].astype(F32) + rx[0, r, :].astype(F32) + rx[1, r, :].astype(F32) + rx[2, r, :].astype(F32)).astype(BF)
    sz = [go(w2.at[lax.rem(zl + k, 8)], rz.at[k - 1], zs.at[k - 1], zr.at[k - 1], zp[k - 1]) for k in range(1, 8)]
    s3 = []
    for h in range(2):
        _, k1h, p2, k2h = plan[h]
        s2[h].wait_recv()
        place_q = (rows_of(k1h), cols_of(h, k2h))
        dwo_ref[place_q] = (k1[h, k2h].astype(F32) + e2[h].astype(F32)).astype(BF)
        s3.append(go(dwo_ref.at[place_q], dwo_ref.at[place_q], es.at[h, 2], er.at[h, 2], p2))
    for c in sz:
        c.wait_recv()
    total = w2[zl].astype(F32)
    for k in range(7):
        total = total + rz[k].astype(F32)
    hs[...] = total[:, 0:1024].astype(BF)
    sh = go(hs, hr, cs.at[1], cr.at[1], other)
    fy[...] = total[:, 1024:1152]
    sy = [go(fy, ry.at[k], ys.at[k], yr.at[k], yp[k]) for k in range(3)]

    def arrived(dst, sem, peer):
        pltpu.make_async_remote_copy(src_ref=dst, dst_ref=dst, send_sem=cs.at[0], recv_sem=sem, device_id=peer, device_id_type=MESH).wait_recv()

    s4 = []
    for h in range(2):
        p1, k1h, p2, k2h = plan[h]
        theirs = (rows_of(k1h), cols_of(h, 1 - k2h))
        arrived(dwo_ref.at[theirs], er.at[h, 2], p2)
        block = (rows_of(k1h), slice(h * 1024, (h + 1) * 1024))
        s4.append(go(dwo_ref.at[block], dwo_ref.at[block], es.at[h, 3], er.at[h, 3], p1))
    for c in sy:
        c.wait_recv()
    at = x * 8 + zl
    fg_ref[core, at] = (fy[...] + ry[0] + ry[1] + ry[2]).astype(BF)
    for k in range(1, 8):
        go(fg_ref.at[core, at], fg_ref.at[core, at], fs.at[k - 1], fr.at[k - 1], zp[k - 1])
    sh.wait_recv()
    mine, theirs = hs[...].astype(F32), hr[...].astype(F32)
    mine = jnp.where(core == 0, mine[0:4], mine[4:8])
    theirs = jnp.where(core == 0, theirs[0:4], theirs[4:8])
    hid_ref[:, 0:1024] = jnp.where(core == 0, mine, theirs).astype(BF)
    hid_ref[:, 1024:2048] = jnp.where(core == 0, theirs, mine).astype(BF)
    for k in range(1, 8):
        arrived(fg_ref.at[core, x * 8 + lax.rem(zl + 8 - k, 8)], fr.at[k - 1], zp[k - 1])
    column = pl.ds(x * 8, 8)
    for k in (1, 2, 3):
        go(fg_ref.at[core, column], fg_ref.at[core, column], fs.at[6 + k], fr.at[6 + k], xp[k - 1])
    for k in (1, 2, 3):
        arrived(fg_ref.at[core, pl.ds(lax.rem(x + 4 - k, 4) * 8, 8)], fr.at[6 + k], xp[k - 1])
    go(fg_ref.at[core], fg_ref.at[core], cs.at[2], cr.at[2], other)
    arrived(fg_ref.at[1 - core], cr.at[2], other)
    for h in range(2):
        p1, k1h, _, _ = plan[h]
        arrived(dwo_ref.at[rows_of(1 - k1h), h * 1024:(h + 1) * 1024], er.at[h, 3], p1)
    for copy in pend:
        copy.wait_send()


DMA = pltpu.SemaphoreType.DMA


def remote(cid, mib=32):
    return pltpu.CompilerParams(collective_id=cid, has_side_effects=True, vmem_limit_bytes=mib << 20)


def states(total):
    return pl.pallas_call(
        states_kernel, out_shape=out(4, 40, 128), in_specs=[V], out_specs=V,
        scratch_shapes=[DMA((3,)), DMA((3,))], compiler_params=remote(1), name="states",
    )(total)


def edges(dpre):
    return pl.pallas_call(
        edges_kernel, out_shape=out(2, 8, 128), in_specs=[V], out_specs=V,
        scratch_shapes=[DMA((2,)), DMA((2,))], compiler_params=remote(2), name="edges",
    )(dpre)


def reduce(gin, dw):
    W = HALF + 128
    vm = pltpu.VMEM
    return pl.pallas_call(
        reduce_kernel,
        out_shape=(out(4, D, dtype=BF), out(192, D, dtype=BF), out(2, 32, 8, 128, dtype=BF)),
        in_specs=[V] * 2, out_specs=[V] * 3,
        scratch_shapes=[
            vm((256, W), BF), vm((4, 64, W), BF), vm((3, 64, W), BF), vm((8, 8, W), BF), vm((7, 8, W), BF),
            vm((8, 1024), BF), vm((8, 1024), BF), vm((8, 128), F32), vm((3, 8, 128), F32),
            vm((2, 96, 1024), BF), vm((2, 2, 96, 512), BF), vm((2, 96, 512), BF),
            DMA((3,)), DMA((3,)), DMA((3,)), DMA((3,)), DMA((7,)), DMA((7,)), DMA((3,)), DMA((3,)), DMA((10,)), DMA((10,)), DMA((2, 4)), DMA((2, 4)),
        ],
        compiler_params=remote(3), name="reduce",
    )(gin, dw)


def local(hidden, w_in, w_bc, w_dt, dt_bias, a_log, d_skip, conv_w, w_out, d_out):
    ctx, tp = lax.axis_index("ctx"), lax.axis_index("tp")
    at = jnp.stack([ctx // 2, tp % 2, ctx % 2, 0]).astype(jnp.int32)
    par = jnp.concatenate([dt_bias, -jnp.exp(a_log), d_skip, jnp.zeros((1,), F32)])
    wcat, w7 = weights(w_in, w_bc, w_dt, conv_w)
    own, oth = gather(hidden, d_out)
    own, oth = own.reshape(2 * EXT, HALF), oth.reshape(2 * EXT, HALF)
    wf, pre, z, dtr, gg, bc, cum, sums, total = prepare(at, par, own, oth, wcat, w_out, w7)
    everything = states(total)
    gated, dpre, dz, tail = scan(at, par, everything, pre, z, dtr, gg, bc, cum, sums)
    edge = edges(dpre)
    gin, dw = finish(at, edge, own, oth, wcat, wf, w7, gated, dpre, dz, tail)
    d_hidden, dw, shared = reduce(gin, dw)
    d_w_in = dw[0:128].T.astype(F32)
    d_w_out = dw[128:192].astype(F32)
    d_w_bc = shared.reshape(2, 8, 32, 128).transpose(0, 1, 3, 2).reshape(D, 2 * 16).astype(F32)
    return (d_hidden, d_w_in, d_w_out, d_w_bc)


def solution(mesh):
    in_specs = (
        P(("ctx", "tp"), None), P(None, "tp"), P(), P("tp", None), P("tp"), P("tp"), P("tp"), P(None, "tp"),
        P("tp", None), P(("ctx", "tp"), None),
    )
    out_specs = (P(("ctx", "tp"), None), P(None, "tp"), P("tp", None), P())
    return jax.shard_map(local, mesh=mesh, in_specs=in_specs, out_specs=out_specs, check_vma=False)
```

time: 1350 us -> 145 us (0.11)
  blocking collectives: 773 us -> 0 us
  waiting for transfers between devices: 380 us -> 0 us
  Pallas kernels: 0 us -> 122 us
  local copies, waits for them, and re-layouts: 87.5 us -> 14.4 us
  other arithmetic: 44.4 us -> 5.26 us
  matrix products: 25.8 us -> 0 us
  between operations: 17.6 us -> 2.75 us
  starting transfers between devices: 13.6 us -> 0 us
    unnamed x2 -> x0, blocking collectives: 540 us -> none
    all_gather x4 -> x0, blocking collectives: 233 us -> none  [entering(): everything = jax.tree.map(lambda part: lax.all_gather(part, axis), array)]
    all_gather x2 -> x0, waiting for transfers between devices: 196 us -> none  [the longest x1 107 us: local(): portion = lax.all_gather(d_out, 'tp', axis=0, tiled=True)]
    psum x2 -> x0, waiting for transfers between devices: 176 us -> none  [the longest x1 176 us: local(): lax.psum((grad_bpair[:, :2 * STATE] + grad_bpair[::-1, 2 * STATE:]) * sca...]
    pallas_call x0 -> x7, Pallas kernels: none -> 122 us  [the longest x1 53 us: gather(): pl.pallas_call(gather_kernel, out_shape=(out, out), in_specs=[pl.BlockSpe...]
    rev x15 -> x1, local copies, waits for them, and re-layouts: 39.6 us -> 0.7 us  [weights(): conv_w[::-1]]
    dot_general x30 -> x0, matrix products: 25.8 us -> none  [the longest x5 6.78 us: block_ssd(): scores = jnp.einsum('in,jn->ij', c_rows, b_rows, precision=precise) * decays]
    select_n x33 -> x0, other arithmetic: 20.9 us -> none  [the longest x32 20.9 us: step(): return jax.tree.map(lambda a, b: jnp.where(reached, a, b), new, before)]
  transfers between devices with their start and end apart: 8 -> 0, of which waited for: 4 -> 0; matrix products, arithmetic and copies ran while one was open for 6% -> 0% of each run, Pallas kernels for 0% -> 0%
where the time goes in v1:
time: 145 us
  Pallas kernels  122 us (84%)
  local copies, waits for them, and re-layouts  14.4 us (10%)
  other arithmetic  5.26 us (4%)
  between operations  2.75 us (2%)
    pallas_call x1, Pallas kernels, gather(): pl.pallas_call(gather_kernel, out_shape=(out, out), in_specs=[pl.BlockSpe...  53 us
    pallas_call x1, Pallas kernels, reduce(): pl.pallas_call(reduce_kernel, out_shape=(out(4, D, dtype=BF), out(192, D,...  39.2 us
    unnamed x24, local copies, waits for them, and re-layouts  11.8 us
    pallas_call x1, Pallas kernels, finish(): pl.pallas_call(finish_kernel, out_shape=(out(2, 256, HALF + 128, dtype=BF...  7.79 us
    pallas_call x1, Pallas kernels, prepare(): pl.pallas_call(prepare_kernel, out_shape=(out(D, 256, dtype=BF), out(ROWS...  6.97 us
    pallas_call x1, Pallas kernels, states(): pl.pallas_call(states_kernel, out_shape=out(4, 40, 128), in_specs=[V], ou...  5.63 us
    pallas_call x1, Pallas kernels, scan(): pl.pallas_call(scan_kernel, out_shape=(out(ROWS, 128), out(ROWS, 128), ou...  5.1 us
    pallas_call x1, Pallas kernels, edges(): pl.pallas_call(edges_kernel, out_shape=out(2, 8, 128), in_specs=[V], out_...  4.44 us

profile of v1, /device:TPU:1, one launch (start us, length us, event | category | flops | bytes accessed | tf_op | source)
XLA Modules:
  0.0 144.5 jit_solution(2396647813888671556)
XLA Ops:
  0.6 0.0 copy-start.9
  0.6 0.0 copy-start.8
  2.7 0.6 pad_add_fusion.at_ref
  3.2 0.6 pad_maximum_fusion.par_ref
  3.8 0.1 pad.8.clone
  3.9 0.7 rev.3
  4.6 0.8 select_maximum_fusion
  5.3 0.6 concatenate.23.w7_ref
  5.9 1.2 copy.17
  7.1 1.0 copy.18
  8.1 2.4 %maximum_maximum_fusion.wcat_ref = bf16[2048,256]{1,0:T(8,128)(2,1)} fusion(bf16[2048,1]{1,0:T(8,128)(2,1)S(1)} %copy.18, bf16[2048,32]{1,0:T(8,128)(2,1)S(1)} %copy.17, bf16[2048,128]{1,0:T(8,128)(2,1)} %param.11, bf16[256]{0:T(256)(128)(2,1)S(1)} %pad.8.clone), kind=kLoop, calls=%fused_computation | loop fusion | flops 4194304 | bytes 1708544 | tf_op jit(solution)/shard_map/concatenate | solution.py:446
  10.6 0.0 copy-done.9
  10.6 0.0 copy-done.8
  10.6 53.0 %gather_rows.1 = (bf16[2,66,8,1024]{3,2,1,0:T(8,128)(2,1)S(1)}, bf16[2,66,8,1024]{3,2,1,0:T(8,128)(2,1)S(1)}) custom-call(bf16[4,2048]{1,0:T(4,128)(2,1)S(1)} %copy-done.8, bf16[4,2048]{1,0:T(4,128)(2,1)S(1)} %copy-done.9), custom_call_target="tpu_custom_call" | custom-call | tf_op jit(solution)/shard_map/gather_rows/pallas_call | solution.py:146
  63.6 0.0 copy-start
  63.6 1.3 copy-done
  64.9 0.0 copy-start.1
  64.9 1.3 copy-done.1
  66.2 7.0 %prepare.1 = (bf16[2048,256]{1,0:T(8,128)(2,1)}, f32[512,128]{1,0:T(8,128)}, f32[512,128]{1,0:T(8,128)}, f32[512,128]{1,0:T(8,128)}, f32[512,128]{1,0:T(8,128)},...) custom-call(s32[4]{0:T(128)} %pad_add_fusion.at_ref, ...), custom_call_target="tpu_custom_call" | custom-call | tf_op jit(solution)/shard_map/prepare/pallas_call | solution.py:416
  73.2 0.0 copy-start.7
  73.2 0.7 copy-done.7
  73.9 5.6 %states.1.all_ref = f32[4,40,128]{2,1,0:T(8,128)S(1)} custom-call(f32[40,128]{1,0:T(8,128)S(1)} %copy-done.7), custom_call_target="tpu_custom_call" | custom-call | tf_op jit(solution)/shard_map/states/pallas_call | solution.py:590
  79.6 0.0 copy-start.5
  79.6 0.6 copy-done.5
  80.2 5.1 %scan.1 = (f32[512,128]{1,0:T(8,128)}, f32[512,128]{1,0:T(8,128)}, f32[512,128]{1,0:T(8,128)}, f32[2,512,128]{2,1,0:T(8,128)}) custom-call(s32[4]{0:T(128)} %pad_add_fusion.at_ref, f32[4]{0:T(128)} %pad_maximum_fusion.par_ref, f32[4,40,128]{2,1,0:T(8,128)} %copy-done.5, f32[512,128]{1,0:T(8,128)} %get-tuple-element.27.pre_ref, ...), custom_call_target="tpu_custom_call" | custom-call | tf_op jit(solution)/shard_map/scan/pallas_call | solution.py:427
  85.3 0.0 copy-start.3
  85.3 0.9 copy-done.3
  86.3 4.4 %edges.1.edge_ref = f32[2,8,128]{2,1,0:T(8,128)S(1)} custom-call(f32[512,128]{1,0:T(8,128)S(1)} %copy-done.3), custom_call_target="tpu_custom_call" | custom-call | tf_op jit(solution)/shard_map/edges/pallas_call | solution.py:597
  90.7 0.0 copy-start.6
  90.7 0.6 copy-done.6
  91.3 7.8 %finish.1 = (bf16[2,256,1152]{2,1,0:T(8,128)(2,1)}, bf16[192,2048]{1,0:T(8,128)(2,1)}) custom-call(s32[4]{0:T(128)} %pad_add_fusion.at_ref, f32[2,8,128]{2,1,0:T(8,128)} %copy-done.6, bf16[1056,1024]{1,0:T(8,128)(2,1)} %bitcast.22, bf16[1056,1024]{1,0:T(8,128)(2,1)} %bitcast.24, bf16[2048,256]{1,0:T(8,128)(2,1)} %maximum_maximum_fusion.wcat_ref, ...), custom_call_target="tpu_custom_call" | custom-call | tf_op jit(solution)/shard_map/finish/pallas_call | solution.py:436
  99.1 0.0 copy-start.2
  99.1 1.3 copy-done.2
  100.4 0.0 copy-start.4
  100.4 1.1 copy-done.4
  101.5 39.2 %reduce.1 = (bf16[4,2048]{1,0:T(4,128)(2,1)S(1)}, bf16[192,2048]{1,0:T(8,128)(2,1)S(1)}, bf16[2,32,8,128]{3,2,1,0:T(8,128)(2,1)S(1)}) custom-call(bf16[2,256,1152]{2,1,0:T(8,128)(2,1)S(1)} %copy-done.2, bf16[192,2048]{1,0:T(8,128)(2,1)S(1)} %copy-done.4), custom_call_target="tpu_custom_call" | custom-call | tf_op jit(solution)/shard_map/reduce/pallas_call | solution.py:606
  140.7 0.2 copy.19
  140.9 0.8 copy.23
  141.7 0.8 slice_convert_fusion
  142.5 0.1 convert_bitcast_fusion
  142.6 1.3 copy.20
  143.9 0.6 copy.28
  (2 shorter events, 0.0 us)
Async XLA Ops:
  0.6 9.9 %copy-start.9 = (bf16[4,2048]{1,0:T(4,128)(2,1)S(1)}, bf16[4,2048]{1,0:T(4,128)(2,1)}, u32[]{:S(2)}) copy-start(bf16[4,2048]{1,0:T(4,128)(2,1)} %g_ref.1) | copy-start | bytes 49156
  0.6 9.9 %copy-start.8 = (bf16[4,2048]{1,0:T(4,128)(2,1)S(1)}, bf16[4,2048]{1,0:T(4,128)(2,1)}, u32[]{:S(2)}) copy-start(bf16[4,2048]{1,0:T(4,128)(2,1)} %h_ref.1) | copy-start | bytes 49156
  63.6 1.4 copy-start
  64.9 1.3 copy-start.1
  73.2 0.7 copy-start.7
  79.6 0.6 copy-start.5
  85.3 0.9 copy-start.3
  90.7 0.6 copy-start.6
  99.1 1.3 copy-start.2
  100.4 1.1 copy-start.4

commit v2 on v0

v2 whole, which is shorter than its diff:
```python
import math

import jax
import jax.numpy as jnp
from jax import lax
from jax.experimental import pallas as pl
from jax.experimental.pallas import tpu as pltpu
from jax.sharding import PartitionSpec as P

MESH = pl.DeviceIdType.MESH
BF, F32 = jnp.bfloat16, jnp.float32
ROWS, EXT, D, HALF, CH = 512, 528, 2048, 1024, 256
SCALING = 1.0 / math.sqrt(D)


def place():
    ctx, tp = lax.axis_index("ctx"), lax.axis_index("tp")
    y, zh = ctx // 2, ctx % 2
    x, zl, core = tp // 16, (tp // 2) % 8, tp % 2
    return x, y, zh * 8 + zl, core


def dev(x, y, z, core):
    return (y * 2 + z // 8, x * 16 + (z % 8) * 2 + core)


def greet(peers):
    barrier = pltpu.get_barrier_semaphore()
    for peer in peers:
        pl.semaphore_signal(barrier, inc=1, device_id=peer, device_id_type=MESH)
    pl.semaphore_wait(barrier, len(peers))


def remote(src, dst, ssem, rsem, peer):
    return pltpu.make_async_remote_copy(src_ref=src, dst_ref=dst, send_sem=ssem, recv_sem=rsem, device_id=peer, device_id_type=MESH)


def mm(a, b, dims):
    return lax.dot_general(a, b, (dims, ((), ())), preferred_element_type=F32)


def nn(a, b):
    return mm(a, b, ((1,), (0,)))


def nt(a, b):
    return mm(a, b, ((1,), (1,)))


def tn(a, b):
    return mm(a, b, ((0,), (0,)))


def iota(shape, dim):
    return lax.broadcasted_iota(jnp.int32, shape, dim)


def ones_where(mask):
    return mask.astype(F32).astype(BF)


def split3(v):
    h = v.astype(BF)
    m = (v - h.astype(F32)).astype(BF)
    l = (v - h.astype(F32) - m.astype(F32)).astype(BF)
    return h, m, l


def exact_left(t, v):
    h, m, l = split3(v)
    return (nn(t, l) + nn(t, m)) + nn(t, h)


def exact_right(v, t):
    h, m, l = split3(v)
    return (nn(l, t) + nn(m, t)) + nn(h, t)


def fwd_lanes(shape):
    return iota(shape, 1) < 64


def softplus(v):
    return jnp.maximum(v, 0.0) + jnp.log1p(jnp.exp(-jnp.abs(v)))


def sigmoid(v):
    return jax.nn.sigmoid(v)


def mixer_kernel(h_ref, g_ref, win_ref, wbc_ref, wdt_ref, bias_ref, alog_ref, skip_ref, conv_ref, wout_ref,
                 hid_ref, dwi_ref, dwo_ref, fg_ref,
                 swap, asm, own, oth, hown, hoth, wcat, wf, wo, x_scr, d_scr,
                 pre_s, z_s, dtr_s, gg_s, bc_s, cum_s, total_s, all_s, gated_s, dpre_s, dz_s, tail_s, edge_s,
                 gcat, acc, dwi, dwo, gin, rc, w1, rx, w2, rz, hs, hr,
                 fb, fc, f1, fx, f2, fz, fy, ry, ei1, ki1, ei2, eo1, ko1, eo2,
                 sw_s, sw_r, zs, zr, xs, xr, cs, cr, ys, yr, hs_s, hs_r, st_s, st_r, ed_s, ed_r,
                 dc_s, dc_r, dx_s, dx_r, dz_ss, dz_rr, fc_s, fc_r, fx_s, fx_r, fz_s, fz_r, fy_s, fy_r, ga_s, ga_r,
                 ei_s, ei_r, eo_s, eo_r):
    x, y, z, core = place()
    zh, zl = z // 8, z % 8
    bias, rate, skip = bias_ref[...], -jnp.exp(alog_ref[...]), skip_ref[...]
    other = dev(x, y, z, 1 - core)
    xp = [dev(lax.rem(x + k, 4), y, z, core) for k in (1, 2, 3)]
    yp = [dev(x, lax.rem(y + k, 4), z, core) for k in (1, 2, 3)]

    def along(k):
        return dev(x, y, lax.rem(z + 16 + k, 16), core)

    def line(k):
        return dev(x, y, zh * 8 + lax.rem(zl + k, 8), core)

    mine = pl.ds(pl.multiple_of(core * HALF, HALF), HALF)
    theirs = pl.ds(pl.multiple_of((1 - core) * HALF, HALF), HALF)
    pend = []

    def go(src, dst, ssem, rsem, peer):
        copy = remote(src, dst, ssem, rsem, peer)
        copy.start()
        pend.append(copy)
        return copy

    def arrived(dst, rsem):
        remote(dst, dst, sw_s.at[0], rsem, other).wait_recv()

    greet([other] + xp + yp + [along(k) for k in (-3, -2, -1, 1, 2, 3)] + [line(k) for k in range(1, 8)])

    go(h_ref.at[:, theirs], swap.at[0], sw_s.at[0], sw_r.at[0], other)
    go(g_ref.at[:, theirs], swap.at[1], sw_s.at[1], sw_r.at[1], other)

    def blk(xx, k):
        zz = lax.rem(z + 16 + k, 16)
        return (zz // 8) * 32 + xx * 8 + zz % 8

    home = blk(x, 0)
    arrived(swap.at[0], sw_r.at[0])
    arrived(swap.at[1], sw_r.at[1])
    for k, ref in ((0, h_ref), (1, g_ref)):
        here, there = ref[:, mine].astype(F32), swap[k].astype(F32)
        asm[0:4, :] = jnp.where(core == 0, here, there)
        asm[4:8, :] = jnp.where(core == 0, there, here)
        own[k, home] = asm[...].astype(BF)

    def slot(k):
        return k if k >= 0 else 7 - k

    def cross(b, n):
        go(own.at[:, b], oth.at[:, b], cs.at[n], cr.at[n], other)

    def carry(k, far):
        b, n = blk(x, k), slot(k - far)
        go(own.at[:, b], own.at[:, b], zs.at[n], zr.at[n], along(far))

    def spread(k):
        b, n = blk(x, k), slot(k)
        for j in (2, 1, 3):
            go(own.at[:, b], own.at[:, b], xs.at[j - 1, n], xr.at[j - 1, n], xp[j - 1])
        cross(b, n)

    def z_arrival(k):
        arrived(own.at[:, blk(x, k)], zr.at[slot(k)])

    def x_arrivals(k):
        n = slot(k)
        for j in (1, 3, 2):
            b = blk(lax.rem(x + 4 - j, 4), k)
            arrived(own.at[:, b], xr.at[j - 1, n])
            cross(b, 16 * j + n)

    for far in (3, -3, 2, -2, 1, -1):
        carry(0, far)
    spread(0)

    flip = ones_where(iota((256, 256), 0) + iota((256, 256), 1) == 255)
    pick = ones_where(iota((8, 128), 1) == jnp.where(iota((8, 128), 0) == 0, 32, -1))
    for q in range(8):
        r, back = slice(q * 256, (q + 1) * 256), slice((7 - q) * 256, (8 - q) * 256)
        wcat[r, 0:128] = win_ref[r, :]
        steps = tn(jnp.broadcast_to(wdt_ref[:, r].astype(F32), (8, 256)).astype(BF), pick)
        shared = jnp.concatenate([wbc_ref[r, :].astype(F32), jnp.zeros((256, 96), F32)], axis=1)
        wcat[r, 128:256] = (shared + steps).astype(BF)
        wo[0:64, r] = wout_ref[:, r]
        wo[64:128, r] = nn(wout_ref[:, back], flip).astype(BF)
    for q in range(8):
        wf[q * 256:(q + 1) * 256, :] = nn(flip, wcat[(7 - q) * 256:(8 - q) * 256, :]).astype(BF)
    gap = jnp.zeros((1, 64), F32)
    taps = []
    for k in range(7):
        f_tap = conv_ref[k:k + 1, :] if k < 4 else gap
        r_tap = conv_ref[6 - k:7 - k, :] if k >= 3 else gap
        taps.append(jnp.concatenate([f_tap, r_tap], axis=1))

    for k in (-3, 3):
        z_arrival(k)
        step = 1 if k < 0 else -1
        for far in (3, 2, 1):
            carry(k, step * far)
    for k in (-3, 3):
        spread(k)
    for k in (-1, 1, -2, 2):
        z_arrival(k)
        spread(k)
    x_arrivals(0)
    for k in (-6, 6):
        z_arrival(k)
        if k < 0:
            carry(k, 2)
            carry(k, 1)
        else:
            carry(k, -1)
    for k in (-6, 6):
        spread(k)
    for k in (-4, 4, -5, 5):
        z_arrival(k)
        spread(k)
    for k in (-3, 3, -1, 1, -2, 2):
        x_arrivals(k)
    for k in (-7, 7, -8):
        z_arrival(k)
        spread(k)
    for k in (-6, 6, -4, 4, -5, 5, -7, 7, -8):
        x_arrivals(k)
    go(own.at[0, 63], hown.at[0], ys.at[0], yr.at[0], yp[0])
    go(own.at[0, 0], hown.at[1], ys.at[1], yr.at[1], yp[2])
    for n in range(64):
        arrived(oth.at[:, 0], cr.at[n])

    h_own, h_oth = own[0].reshape(ROWS, HALF), oth[0].reshape(ROWS, HALF)
    g_own, g_oth = own[1].reshape(ROWS, HALF), oth[1].reshape(ROWS, HALF)
    gg = nt(g_own, wo[:, mine]) + nt(g_oth, wo[:, theirs])
    gg_s[...] = gg
    for j in range(2):
        arrived(hown.at[j], yr.at[j])
        go(hown.at[j], hoth.at[j], hs_s.at[j], hs_r.at[j], other)
    pf = nn(h_own, wcat[mine, :]) + nn(h_oth, wcat[theirs, :])
    pr = nn(h_own, wf[mine, :]) + nn(h_oth, wf[theirs, :])
    lanes = fwd_lanes((ROWS, 128))
    x2 = jnp.where(lanes, pf[:, 0:128], pltpu.roll(pr[:, 0:128], 64, 1)).astype(BF).astype(F32)
    z2 = jnp.where(lanes, pltpu.roll(pf[:, 0:128], 64, 1), pr[:, 0:128]).astype(BF).astype(F32)
    x_scr[8:8 + ROWS, :] = x2
    z_s[...] = z2
    bf, br = pf[:, 128:256], pr[:, 128:256]
    bc_s[0] = bf.astype(BF)
    bc_s[1] = br.astype(BF)
    dtr = jnp.where(lanes, bf[:, 32:33], br[:, 32:33]) + bias
    dtr_s[...] = dtr
    dt = softplus(dtr)
    la = dt * rate
    dy = gg * (z2 * sigmoid(z2))
    for j in range(2):
        arrived(hoth.at[j], hs_r.at[j])
    e_own, e_oth = hown[...].reshape(16, HALF), hoth[...].reshape(16, HALF)
    xf = nn(e_own, wcat[mine, 0:128]) + nn(e_oth, wcat[theirs, 0:128])
    xb = nn(e_own, wf[mine, 0:128]) + nn(e_oth, wf[theirs, 0:128])
    edge = jnp.where(fwd_lanes((16, 128)), xf, pltpu.roll(xb, 64, 1)).astype(BF).astype(F32)
    x_scr[0:8, :] = jnp.where(y == 0, 0.0, edge[0:8])
    x_scr[8 + ROWS:EXT, :] = jnp.where(y == 3, 0.0, edge[8:16])
    pre = taps[0] * x_scr[5:5 + ROWS, :]
    for k in range(1, 7):
        pre = pre + taps[k] * x_scr[5 + k:5 + k + ROWS, :]
    pre_s[...] = pre
    u = dt * (pre * sigmoid(pre))

    low = ones_where(iota((CH, CH), 0) >= iota((CH, CH), 1))
    upp = ones_where(iota((CH, CH), 0) <= iota((CH, CH), 1))
    lanes, lane1, lane16 = fwd_lanes((CH, 128)), fwd_lanes((1, 128)), fwd_lanes((16, 128))
    ends, sts, ads = [], [], []
    for c in range(2):
        rows = slice(c * CH, (c + 1) * CH)
        cum = jnp.where(lanes, exact_left(low, la[rows]), exact_left(upp, la[rows]))
        cum_s[rows, :] = cum
        end = jnp.where(lane1, cum[CH - 1:CH], cum[0:1])
        ru = (jnp.exp(end - cum) * u[rows]).astype(BF)
        ed = (jnp.exp(cum) * dy[rows]).astype(BF)
        b0, b1 = bf[rows].astype(BF), br[rows].astype(BF)
        sts.append(jnp.where(lane16, tn(b0, ru)[0:16], tn(b1, ru)[0:16]))
        ads.append(jnp.where(lane16, tn(b0, ed)[16:32], tn(b1, ed)[16:32]))
        ends.append(end)
    e0, e1 = jnp.exp(ends[0]), jnp.exp(ends[1])
    total_s[0:16, :] = jnp.where(lane16, e1 * sts[0] + sts[1], e0 * sts[1] + sts[0])
    total_s[16:32, :] = jnp.where(lane16, ads[0] + e0 * ads[1], ads[1] + e1 * ads[0])
    total_s[32:40, :] = jnp.broadcast_to(jnp.exp(ends[0] + ends[1]), (8, 128))
    all_s[y] = total_s[...]
    for k in range(3):
        go(total_s, all_s.at[y], st_s.at[k], st_r.at[k], yp[k])
    for k in range(3):
        arrived(all_s.at[lax.rem(y + 3 - k, 4)], st_r.at[k])
    nil = jnp.zeros((16, 128), F32)
    s_f, s_r, e_f, e_r = nil, nil, nil, nil
    for k in range(4):
        st, ad, dk = all_s[k, 0:16, :], all_s[k, 16:32, :], all_s[k, 32:33, :]
        s_f = jnp.where(k < y, dk * s_f + st, s_f)
        e_r = jnp.where(k < y, dk * e_r + ad, e_r)
    for k in (3, 2, 1, 0):
        st, ad, dk = all_s[k, 0:16, :], all_s[k, 16:32, :], all_s[k, 32:33, :]
        s_r = jnp.where(k > y, dk * s_r + st, s_r)
        e_f = jnp.where(k > y, dk * e_f + ad, e_f)
    state, adj = jnp.where(lane16, s_f, s_r), jnp.where(lane16, e_f, e_r)
    s_in = [jnp.where(lane16, state, e1 * state + sts[1]), jnp.where(lane16, e0 * state + sts[0], state)]
    e_out = [jnp.where(lane16, ads[1] + e1 * adj, adj), jnp.where(lane16, adj, ads[0] + e0 * adj)]
    s_out = [e0 * s_in[0] + sts[0], e1 * s_in[1] + sts[1]]

    same = ones_where((iota((128, 128), 0) < 64) == (iota((128, 128), 1) < 64))
    ii, jj = iota((CH, CH), 0), iota((CH, CH), 1)
    for c in range(2):
        rows = slice(c * CH, (c + 1) * CH)
        pre, zz, dtr, gg, cum = (r[rows, :] for r in (pre_s, z_s, dtr_s, gg_s, cum_s))
        sg, sz = sigmoid(pre), sigmoid(zz)
        xc, gate = pre * sg, zz * sz
        dt = softplus(dtr)
        u, dy = dt * xc, gg * gate
        ub, dyb = u.astype(BF), dy.astype(BF)
        rem, grow = jnp.exp(ends[c] - cum), jnp.exp(cum)
        cum_t = cum.T
        sb, eb = s_in[c].astype(BF), e_out[c].astype(BF)
        y_s, du_s, tails = [], [], []
        for s in range(2):
            bc = bc_s[s, rows, :]
            b, cc = bc[:, 0:16], bc[:, 16:32]
            col, across = cum[:, 64 * s:64 * s + 1], cum_t[64 * s:64 * s + 1, :]
            mask = (ii >= jj) if s == 0 else (ii <= jj)
            decay = jnp.exp(jnp.where(mask, col - across, -1e30))
            w = (nt(cc, b) * decay).astype(BF)
            rem_c, grow_c = rem[:, 64 * s:64 * s + 1], grow[:, 64 * s:64 * s + 1]
            y_s.append(nn(w, ub) + grow_c * nn(cc, sb))
            du_s.append(tn(w, dyb) + rem_c * nn(b, eb))
            half = lanes if s == 0 else jnp.logical_not(lanes)
            dym = jnp.where(half, dy, 0.0).astype(BF)
            um = jnp.where(half, u, 0.0).astype(BF)
            ds = (nt(dym, ub) * decay).astype(BF)
            dc = nn(ds, b) + grow_c * nt(dym, sb)
            db = tn(ds, cc) + rem_c * nt(um, eb)
            tails.append((db, dc))
        y2, du = jnp.where(lanes, y_s[0], y_s[1]), jnp.where(lanes, du_s[0], du_s[1])
        dl = exact_right(dyb.astype(F32) * y2 - ub.astype(F32) * du, same)
        direct = exact_right(du * xc, same)
        const = jnp.sum(e_out[c] * s_out[c], axis=0, keepdims=True)
        const = exact_right(jnp.broadcast_to(const, (16, 128)), same)[0:1]
        dla = jnp.where(lanes, exact_left(upp, dl), exact_left(low, dl)) + const
        ddt = (rate * dla + direct) * sigmoid(dtr)
        full = y2 + skip * xc
        gated_s[rows, :] = (full * gate).astype(BF)
        dz_s[rows, :] = gg * full * (sz * (1.0 + zz * (1.0 - sz)))
        dpre_s[rows, :] = (du * dt + skip * dy) * (sg * (1.0 + pre * (1.0 - sg)))
        for s in range(2):
            db, dc = tails[s]
            tail = jnp.concatenate([db, dc, ddt[:, 64 * s:64 * s + 1], jnp.zeros((CH, 95), F32)], axis=1).astype(BF)
            tail_s[rows, s * 128:(s + 1) * 128] = tail
            gcat[rows, s * 256 + 128:(s + 1) * 256] = tail

    go(dpre_s.at[ROWS - 8:ROWS, :], edge_s.at[0], ed_s.at[0], ed_r.at[0], yp[0])
    go(dpre_s.at[0:8, :], edge_s.at[1], ed_s.at[1], ed_r.at[1], yp[2])

    near, far = dev(x, y + 1 - 2 * lax.rem(y, 2), z, core), dev(x, 3 - y, z, core)
    turn, side = lax.rem((y + 1) // 2, 2), y // 2
    plan = ((near, turn, far, side), (far, side, near, turn))

    class Sum:
        def __init__(self, src, ref, size, b1, k1, b2, ss, rs):
            self.src, self.ref, self.size, self.b1, self.k1, self.b2, self.ss, self.rs = src, ref, size, b1, k1, b2, ss, rs

        def rows(self, k):
            return pl.ds(pl.multiple_of(k * self.size, self.size), self.size)

        def cols(self, h, k):
            return pl.ds(pl.multiple_of(h * 1024 + k * 512, 512), 512)

        def first(self):
            for h in range(2):
                p1, k1, _, _ = plan[h]
                go(self.src.at[self.rows(1 - k1), h * 1024:(h + 1) * 1024], self.b1.at[h], self.ss.at[h, 0], self.rs.at[h, 0], p1)

        def second(self):
            for h in range(2):
                _, k1, p2, k2 = plan[h]
                arrived(self.b1.at[h], self.rs.at[h, 0])
                for q in range(2):
                    c = slice(h * 1024 + q * 512, h * 1024 + (q + 1) * 512)
                    self.k1[h, q] = (self.src[self.rows(k1), c].astype(F32) + self.b1[h, :, q * 512:(q + 1) * 512].astype(F32)).astype(BF)
                go(self.k1.at[h, 1 - k2], self.b2.at[h], self.ss.at[h, 1], self.rs.at[h, 1], p2)

        def third(self):
            for h in range(2):
                _, k1, p2, k2 = plan[h]
                arrived(self.b2.at[h], self.rs.at[h, 1])
                at = (self.rows(k1), self.cols(h, k2))
                self.ref[at] = (self.k1[h, k2].astype(F32) + self.b2[h].astype(F32)).astype(BF)
                go(self.ref.at[at], self.ref.at[at], self.ss.at[h, 2], self.rs.at[h, 2], p2)

        def fourth(self):
            for h in range(2):
                p1, k1, _, k2 = plan[h]
                arrived(self.ref.at[self.rows(k1), self.cols(h, 1 - k2)], self.rs.at[h, 2])
                at = (self.rows(k1), slice(h * 1024, (h + 1) * 1024))
                go(self.ref.at[at], self.ref.at[at], self.ss.at[h, 3], self.rs.at[h, 3], p1)

        def last(self):
            for h in range(2):
                _, k1, _, _ = plan[h]
                arrived(self.ref.at[self.rows(1 - k1), h * 1024:(h + 1) * 1024], self.rs.at[h, 3])

    s_out_w = Sum(dwo, dwo_ref, 32, eo1, ko1, eo2, eo_s, eo_r)
    s_in_w = Sum(dwi, dwi_ref, 64, ei1, ki1, ei2, ei_s, ei_r)

    acc[0:128, mine] = tn(gated_s[...], own[1].reshape(ROWS, HALF))
    acc[0:128, theirs] = tn(gated_s[...], oth[1].reshape(ROWS, HALF))
    for q in range(8):
        c, back = slice(q * 256, (q + 1) * 256), slice((7 - q) * 256, (8 - q) * 256)
        dwo[:, c] = ((acc[0:64, c] + nn(acc[64:128, back].astype(BF), flip)) * SCALING).astype(BF)
    s_out_w.first()

    acc[:, mine] = tn(tail_s[...], own[0].reshape(ROWS, HALF))
    acc[:, theirs] = tn(tail_s[...], oth[0].reshape(ROWS, HALF))
    for q in range(8):
        c, back = slice(q * 256, (q + 1) * 256), slice((7 - q) * 256, (8 - q) * 256)
        wb = ((acc[0:32, c] + nn(acc[128:160, back].astype(BF), flip)) * SCALING).astype(BF)
        m = (q % 4) * 2
        fb[q // 4, m * 32:(m + 1) * 32, :] = wb[:, 0:128]
        fb[q // 4, (m + 1) * 32:(m + 2) * 32, :] = wb[:, 128:256]
    go(fb.at[1 - core], fc, fc_s.at[0], fc_r.at[0], other)

    d_scr[8:8 + ROWS, :] = dpre_s[...]
    for j in range(2):
        arrived(edge_s.at[j], ed_r.at[j])
    d_scr[0:8, :] = jnp.where(y == 0, 0.0, edge_s[0])
    d_scr[8 + ROWS:EXT, :] = jnp.where(y == 3, 0.0, edge_s[1])
    dx = taps[6] * d_scr[5:5 + ROWS, :]
    for k in range(1, 7):
        dx = dx + taps[6 - k] * d_scr[5 + k:5 + k + ROWS, :]
    dz = dz_s[...]
    lanes = fwd_lanes((ROWS, 128))
    gcat[:, 0:128] = jnp.where(lanes, dx, pltpu.roll(dz, 64, 1)).astype(BF)
    gcat[:, 256:384] = jnp.where(lanes, pltpu.roll(dx, 64, 1), dz).astype(BF)

    arrived(fc, fc_r.at[0])
    for k in range(4):
        f1[k] = (fb[core, k * 64:(k + 1) * 64, :].astype(F32) + fc[k * 64:(k + 1) * 64, :].astype(F32)).astype(BF)
    for k in (1, 2, 3):
        go(f1.at[lax.rem(x + k, 4)], fx.at[k - 1], fx_s.at[k - 1], fx_r.at[k - 1], xp[k - 1])
    s_out_w.second()

    near_rows = pl.ds(pl.multiple_of(zh * 256, 256), 256)
    g_f, g_r = gcat[near_rows, 0:256], gcat[near_rows, 256:512]
    gin[0] = (nt(g_f, wcat[theirs, :]) + nt(g_r, wf[theirs, :])).astype(BF)
    go(gin.at[0], rc, dc_s.at[0], dc_r.at[0], other)
    gin[1] = (nt(g_f, wcat[mine, :]) + nt(g_r, wf[mine, :])).astype(BF)
    for k in (1, 2, 3):
        arrived(fx.at[k - 1], fx_r.at[k - 1])
    for k in range(8):
        r = slice(k * 8, (k + 1) * 8)
        f2[k] = (f1[x, r, :].astype(F32) + fx[0, r, :].astype(F32) + fx[1, r, :].astype(F32) + fx[2, r, :].astype(F32)).astype(BF)
    for k in range(1, 8):
        go(f2.at[lax.rem(zl + k, 8)], fz.at[k - 1], fz_s.at[k - 1], fz_r.at[k - 1], line(k))
    arrived(rc, dc_r.at[0])
    for k in range(4):
        w1[k] = (gin[1, k * 64:(k + 1) * 64, :].astype(F32) + rc[k * 64:(k + 1) * 64, :].astype(F32)).astype(BF)
    for k in (2, 1, 3):
        go(w1.at[lax.rem(x + k, 4)], rx.at[k - 1], dx_s.at[k - 1], dx_r.at[k - 1], xp[k - 1])
    s_out_w.third()

    both = jnp.concatenate([gcat[:, 0:128], gcat[:, 256:384]], axis=1)
    acc[:, mine] = tn(both, own[0].reshape(ROWS, HALF))
    acc[:, theirs] = tn(both, oth[0].reshape(ROWS, HALF))
    for q in range(8):
        c, back = slice(q * 256, (q + 1) * 256), slice((7 - q) * 256, (8 - q) * 256)
        dwi[:, c] = ((acc[0:128, c] + nn(acc[128:256, back].astype(BF), flip)) * SCALING).astype(BF)
    s_in_w.first()
    s_out_w.fourth()
    for k in range(1, 8):
        arrived(fz.at[k - 1], fz_r.at[k - 1])
    part = f2[zl].astype(F32)
    for k in range(7):
        part = part + fz[k].astype(F32)
    fy[...] = part
    for k in range(3):
        go(fy, ry.at[k], fy_s.at[k], fy_r.at[k], yp[k])
    s_in_w.second()
    for k in (1, 3, 2):
        arrived(rx.at[k - 1], dx_r.at[k - 1])
    for k in range(8):
        r = slice(k * 8, (k + 1) * 8)
        w2[k] = (w1[x, r, :].astype(F32) + rx[0, r, :].astype(F32) + rx[1, r, :].astype(F32) + rx[2, r, :].astype(F32)).astype(BF)
    for k in (4, 5, 3, 6, 2, 7, 1):
        go(w2.at[lax.rem(zl + k, 8)], rz.at[k - 1], dz_ss.at[k - 1], dz_rr.at[k - 1], line(k))
    for k in range(3):
        arrived(ry.at[k], fy_r.at[k])
    at = x * 8 + zl
    fg_ref[core, at] = (fy[...] + ry[0] + ry[1] + ry[2]).astype(BF)
    for k in range(1, 8):
        go(fg_ref.at[core, at], fg_ref.at[core, at], ga_s.at[k - 1], ga_r.at[k - 1], line(k))
    s_in_w.third()
    for k in range(1, 8):
        arrived(fg_ref.at[core, x * 8 + lax.rem(zl + 8 - k, 8)], ga_r.at[k - 1])
    column = pl.ds(x * 8, 8)
    for k in (1, 2, 3):
        go(fg_ref.at[core, column], fg_ref.at[core, column], ga_s.at[6 + k], ga_r.at[6 + k], xp[k - 1])
    for k in range(1, 8):
        arrived(rz.at[k - 1], dz_rr.at[k - 1])
    hid = w2[zl].astype(F32)
    for k in range(7):
        hid = hid + rz[k].astype(F32)
    hs[...] = hid.astype(BF)
    go(hs, hr, dc_s.at[1], dc_r.at[1], other)
    s_in_w.fourth()
    for k in (1, 2, 3):
        arrived(fg_ref.at[core, pl.ds(lax.rem(x + 4 - k, 4) * 8, 8)], ga_r.at[6 + k])
    go(fg_ref.at[core], fg_ref.at[core], fc_s.at[1], fc_r.at[1], other)
    arrived(hr, dc_r.at[1])
    a, b = hs[...].astype(F32), hr[...].astype(F32)
    a, b = jnp.where(core == 0, a[0:4], a[4:8]), jnp.where(core == 0, b[0:4], b[4:8])
    hid_ref[:, 0:1024] = jnp.where(core == 0, a, b).astype(BF)
    hid_ref[:, 1024:2048] = jnp.where(core == 0, b, a).astype(BF)
    arrived(fg_ref.at[1 - core], fc_r.at[1])
    s_out_w.last()
    s_in_w.last()
    for copy in pend:
        copy.wait_send()


def mixer(*args):
    def bf(*shape):
        return pltpu.VMEM(shape, BF)

    def f32(*shape):
        return pltpu.VMEM(shape, F32)

    def sems(*shape):
        return [pltpu.SemaphoreType.DMA(shape)] * 2

    def out(*shape):
        return jax.ShapeDtypeStruct(shape, BF)

    V = pl.BlockSpec(memory_space=pltpu.VMEM)
    scratch = [
        bf(2, 4, HALF), f32(8, HALF), bf(2, 64, 8, HALF), bf(2, 64, 8, HALF), bf(2, 8, HALF), bf(2, 8, HALF),
        bf(D, 256), bf(D, 256), bf(128, D), f32(EXT, 128), f32(EXT, 128),
        f32(ROWS, 128), f32(ROWS, 128), f32(ROWS, 128), f32(ROWS, 128), bf(2, ROWS, 128), f32(ROWS, 128),
        f32(40, 128), f32(4, 40, 128), bf(ROWS, 128), f32(ROWS, 128), f32(ROWS, 128), bf(ROWS, 256), f32(2, 8, 128),
        bf(ROWS, 512), f32(256, D), bf(128, D), bf(64, D), bf(2, 256, HALF), bf(256, HALF), bf(4, 64, HALF), bf(3, 64, HALF), bf(8, 8, HALF), bf(7, 8, HALF),
        bf(8, HALF), bf(8, HALF),
        bf(2, 256, 128), bf(256, 128), bf(4, 64, 128), bf(3, 64, 128), bf(8, 8, 128), bf(7, 8, 128), f32(8, 128), f32(3, 8, 128),
        bf(2, 64, 1024), bf(2, 2, 64, 512), bf(2, 64, 512), bf(2, 32, 1024), bf(2, 2, 32, 512), bf(2, 32, 512),
        *sems(2), *sems(16), *sems(3, 16), *sems(64), *sems(2), *sems(2), *sems(3), *sems(2),
        *sems(2), *sems(3), *sems(7), *sems(2), *sems(3), *sems(7), *sems(3), *sems(10), *sems(2, 4), *sems(2, 4),
    ]
    return pl.pallas_call(
        mixer_kernel,
        out_shape=(out(4, D), out(128, D), out(64, D), out(2, 32, 8, 128)),
        in_specs=[V] * 10, out_specs=[V] * 4, scratch_shapes=scratch,
        compiler_params=pltpu.CompilerParams(collective_id=0, has_side_effects=True, vmem_limit_bytes=56 << 20),
        name="mixer",
    )(*args)


def local(hidden, w_in, w_bc, w_dt, dt_bias, a_log, d_skip, conv_w, w_out, d_out):
    one = (1, 1)
    d_hidden, dwi, dwo, shared = mixer(
        hidden, d_out, w_in, w_bc, w_dt, dt_bias.reshape(one), a_log.reshape(one), d_skip.reshape(one), conv_w, w_out
    )
    d_w_bc = shared.reshape(2, 8, 32, 128).transpose(0, 1, 3, 2).reshape(D, 2 * 16).astype(F32)
    return (d_hidden, dwi.T.astype(F32), dwo.astype(F32), d_w_bc)


def solution(mesh):
    in_specs = (
        P(("ctx", "tp"), None), P(None, "tp"), P(), P("tp", None), P("tp"), P("tp"), P("tp"), P(None, "tp"),
        P("tp", None), P(("ctx", "tp"), None),
    )
    out_specs = (P(("ctx", "tp"), None), P(None, "tp"), P("tp", None), P())
    return jax.shard_map(local, mesh=mesh, in_specs=in_specs, out_specs=out_specs, check_vma=False)
```

time: 1350 us -> 104 us (0.08)
  blocking collectives: 773 us -> 0 us
  waiting for transfers between devices: 380 us -> 0 us
  Pallas kernels: 0 us -> 94 us
  local copies, waits for them, and re-layouts: 87.5 us -> 4.93 us
  other arithmetic: 44.4 us -> 1.98 us
  matrix products: 25.8 us -> 0 us
  between operations: 17.6 us -> 2.62 us
  starting transfers between devices: 13.6 us -> 0 us
    unnamed x2 -> x0, blocking collectives: 540 us -> none
    all_gather x4 -> x0, blocking collectives: 233 us -> none  [entering(): everything = jax.tree.map(lambda part: lax.all_gather(part, axis), array)]
    all_gather x2 -> x0, waiting for transfers between devices: 196 us -> none  [the longest x1 107 us: local(): portion = lax.all_gather(d_out, 'tp', axis=0, tiled=True)]
    psum x2 -> x0, waiting for transfers between devices: 176 us -> none  [the longest x1 176 us: local(): lax.psum((grad_bpair[:, :2 * STATE] + grad_bpair[::-1, 2 * STATE:]) * sca...]
    pallas_call x0 -> x1, Pallas kernels: none -> 94 us  [mixer(): pl.pallas_call(mixer_kernel, out_shape=(out(4, D), out(128, D), out(64, D...]
    rev x15 -> x0, local copies, waits for them, and re-layouts: 39.6 us -> none  [the longest x1 8.4 us: local(): out_pair = jnp.concatenate([w_out, w_out[:, ::-1]], axis=0)]
    dot_general x30 -> x0, matrix products: 25.8 us -> none  [the longest x5 6.78 us: block_ssd(): scores = jnp.einsum('in,jn->ij', c_rows, b_rows, precision=precise) * decays]
    select_n x33 -> x0, other arithmetic: 20.9 us -> none  [the longest x32 20.9 us: step(): return jax.tree.map(lambda a, b: jnp.where(reached, a, b), new, before)]
  transfers between devices with their start and end apart: 8 -> 0, of which waited for: 4 -> 0; matrix products, arithmetic and copies ran while one was open for 6% -> 0% of each run, Pallas kernels for 0% -> 0%
where the time goes in v2:
time: 104 us
  Pallas kernels  94 us (90%)
  local copies, waits for them, and re-layouts  4.93 us (5%)
  between operations  2.62 us (3%)
  other arithmetic  1.98 us (2%)
    pallas_call x1, Pallas kernels, mixer(): pl.pallas_call(mixer_kernel, out_shape=(out(4, D), out(128, D), out(64, D...  94 us
    unnamed x10, local copies, waits for them, and re-layouts  4.77 us

profile of v2, /device:TPU:1, one launch (start us, length us, event | category | flops | bytes accessed | tf_op | source)
XLA Modules:
  0.0 103.5 jit_solution(11408282572313164774)
XLA Ops:
  0.6 1.9 %copy.14.wbc_ref = bf16[2048,32]{1,0:T(8,128)(2,1)} copy(bf16[2048,32]{0,1:T(8,128)(2,1)} %param.12) | data formatting | bytes 262144 | tf_op args[2]
  4.5 94.0 %mixer.1 = (bf16[4,2048]{1,0:T(4,128)(2,1)}, bf16[128,2048]{1,0:T(8,128)(2,1)}, bf16[64,2048]{1,0:T(8,128)(2,1)}, bf16[2,32,8,128]{3,2,1,0:T(8,128)(2,1)}) custom-call(bf16[4,2048]{1,0:T(4,128)(2,1)} %h_ref.1, bf16[4,2048]{1,0:T(4,128)(2,1)} %g_ref.1, bf16[2048,128]{1,0:T(8,128)(2,1)} %win_ref.1, bf16[2048,32]{1,0:T(8,128)(2,1)} %copy.14.wbc_ref, ...), custom_call_target="tpu_custom_call" | custom-call | tf_op jit(solution)/shard_map/mixer/pallas_call | solution.py:546
  98.5 1.1 %convert_bitcast_fusion = f32[2048,128]{0,1:T(8,128)S(1)} fusion(bf16[128,2048]{1,0:T(8,128)(2,1)} %get-tuple-element.9), kind=kLoop, calls=%fused_computation | loop fusion | flops 262144 | bytes 1572864 | tf_op jit(solution)/shard_map/convert_element_type | solution.py:561
  99.6 0.0 copy-start.1
  99.7 1.3 %copy.16 = f32[2048,128]{1,0:T(8,128)} copy(f32[2048,128]{0,1:T(8,128)S(1)} %convert_bitcast_fusion) | data formatting | bytes 2097152
  101.0 0.0 copy-done.1
  101.0 0.2 copy.15
  101.2 0.0 copy-start
  101.2 0.8 copy.19
  102.0 0.2 copy-done
  102.1 0.0 copy-start.2
  102.1 0.8 convert_element_type.23
  102.9 0.0 copy-done.2
  102.9 0.6 copy.24
  (1 shorter events, 0.0 us)
Async XLA Ops:
  99.6 1.3 %copy-start.1 = (bf16[2,32,8,128]{3,2,1,0:T(8,128)(2,1)S(1)}, bf16[2,32,8,128]{3,2,1,0:T(8,128)(2,1)}, u32[]{:S(2)}) copy-start(bf16[2,32,8,128]{3,2,1,0:T(8,128)(2,1)} %get-tuple-element.11) | copy-start | bytes 393220
  101.2 1.0 copy-start
  102.1 0.8 copy-start.2

commit v3 on v2

--- a/solution.py
+++ b/solution.py
@@ -88,18 +88,19 @@
     return jax.nn.sigmoid(v)
 
 
-def mixer_kernel(h_ref, g_ref, win_ref, wbc_ref, wdt_ref, bias_ref, alog_ref, skip_ref, conv_ref, wout_ref,
-                 hid_ref, dwi_ref, dwo_ref, fg_ref,
-                 swap, asm, own, oth, hown, hoth, wcat, wf, wo, x_scr, d_scr,
+def mixer_kernel(h_hbm, g_hbm, win_hbm, wbc_hbm, wdt_hbm, bias_ref, alog_ref, skip_ref, conv_hbm, wout_hbm,
+                 hid_ref, dwi_ref, dwo_ref, shared_ref,
+                 h_ref, g_ref, win_ref, wbc_ref, wdt_ref, conv_ref, wout_ref, in_sem, swap, asm, own, oth, hown, hoth, wcat, wf, wo, x_scr, d_scr,
                  pre_s, z_s, dtr_s, gg_s, bc_s, cum_s, total_s, all_s, gated_s, dpre_s, dz_s, tail_s, edge_s,
-                 gcat, acc, dwi, dwo, gin, rc, w1, rx, w2, rz, hs, hr,
+                 gcat, acc, dwi, dwi_sum, dwo, fg, gin, rc, w1, rx, w2, rz, hs, hr,
                  fb, fc, f1, fx, f2, fz, fy, ry, ei1, ki1, ei2, eo1, ko1, eo2,
                  sw_s, sw_r, zs, zr, xs, xr, cs, cr, ys, yr, hs_s, hs_r, st_s, st_r, ed_s, ed_r,
                  dc_s, dc_r, dx_s, dx_r, dz_ss, dz_rr, fc_s, fc_r, fx_s, fx_r, fz_s, fz_r, fy_s, fy_r, ga_s, ga_r,
                  ei_s, ei_r, eo_s, eo_r):
     x, y, z, core = place()
     zh, zl = z // 8, z % 8
-    bias, rate, skip = bias_ref[...], -jnp.exp(alog_ref[...]), skip_ref[...]
+    bias, skip = bias_ref[0], skip_ref[0]
+    rate = -jnp.exp(jnp.full((1, 128), alog_ref[0], F32))
     other = dev(x, y, z, 1 - core)
     xp = [dev(lax.rem(x + k, 4), y, z, core) for k in (1, 2, 3)]
     yp = [dev(x, lax.rem(y + k, 4), z, core) for k in (1, 2, 3)]
@@ -123,8 +124,14 @@
     def arrived(dst, rsem):
         remote(dst, dst, sw_s.at[0], rsem, other).wait_recv()
 
+    loads = []
+    for src, dst in ((h_hbm, h_ref), (g_hbm, g_ref), (wdt_hbm, wdt_ref), (conv_hbm, conv_ref), (wbc_hbm, wbc_ref), (win_hbm, win_ref), (wout_hbm, wout_ref)):
+        loads.append(pltpu.make_async_copy(src, dst, in_sem.at[len(loads)]))
+        loads[-1].start()
     greet([other] + xp + yp + [along(k) for k in (-3, -2, -1, 1, 2, 3)] + [line(k) for k in range(1, 8)])
 
+    loads[0].wait()
+    loads[1].wait()
     go(h_ref.at[:, theirs], swap.at[0], sw_s.at[0], sw_r.at[0], other)
     go(g_ref.at[:, theirs], swap.at[1], sw_s.at[1], sw_r.at[1], other)
 
@@ -153,8 +160,8 @@
 
     def spread(k):
         b, n = blk(x, k), slot(k)
-        for j in (2, 1, 3):
-            go(own.at[:, b], own.at[:, b], xs.at[j - 1, n], xr.at[j - 1, n], xp[j - 1])
+        go(own.at[:, b], own.at[:, b], xs.at[0, n], xr.at[0, n], xp[0])
+        go(own.at[:, b], own.at[:, b], xs.at[1, n], xr.at[1, n], xp[2])
         cross(b, n)
 
     def z_arrival(k):
@@ -162,23 +169,34 @@
 
     def x_arrivals(k):
         n = slot(k)
-        for j in (1, 3, 2):
-            b = blk(lax.rem(x + 4 - j, 4), k)
-            arrived(own.at[:, b], xr.at[j - 1, n])
-            cross(b, 16 * j + n)
+        b = blk(lax.rem(x + 3, 4), k)
+        arrived(own.at[:, b], xr.at[0, n])
+        go(own.at[0, b], own.at[0, b], xs.at[2, n], xr.at[2, n], xp[0])
+        cross(b, 16 + n)
+        b = blk(lax.rem(x + 1, 4), k)
+        arrived(own.at[:, b], xr.at[1, n])
+        go(own.at[1, b], own.at[1, b], xs.at[3, n], xr.at[3, n], xp[2])
+        cross(b, 32 + n)
+
+    def far_arrival(k):
+        n, b = slot(k), blk(lax.rem(x + 2, 4), k)
+        arrived(own.at[0, b], xr.at[2, n])
+        arrived(own.at[1, b], xr.at[3, n])
+        cross(b, 48 + n)
 
     for far in (3, -3, 2, -2, 1, -1):
         carry(0, far)
     spread(0)
 
+    for copy in loads[2:]:
+        copy.wait()
     flip = ones_where(iota((256, 256), 0) + iota((256, 256), 1) == 255)
-    pick = ones_where(iota((8, 128), 1) == jnp.where(iota((8, 128), 0) == 0, 32, -1))
+    pick = ones_where((iota((40, 128), 1) == iota((40, 128), 0)) & (iota((40, 128), 0) < 33))
     for q in range(8):
         r, back = slice(q * 256, (q + 1) * 256), slice((7 - q) * 256, (8 - q) * 256)
         wcat[r, 0:128] = win_ref[r, :]
-        steps = tn(jnp.broadcast_to(wdt_ref[:, r].astype(F32), (8, 256)).astype(BF), pick)
-        shared = jnp.concatenate([wbc_ref[r, :].astype(F32), jnp.zeros((256, 96), F32)], axis=1)
-        wcat[r, 128:256] = (shared + steps).astype(BF)
+        shared = jnp.concatenate([wbc_ref[:, r].astype(F32), jnp.broadcast_to(wdt_ref[:, r].astype(F32), (8, 256))], axis=0)
+        wcat[r, 128:256] = tn(shared.astype(BF), pick).astype(BF)
         wo[0:64, r] = wout_ref[:, r]
         wo[64:128, r] = nn(wout_ref[:, back], flip).astype(BF)
     for q in range(8):
@@ -192,34 +210,38 @@
 
     for k in (-3, 3):
         z_arrival(k)
-        step = 1 if k < 0 else -1
         for far in (3, 2, 1):
-            carry(k, step * far)
-    for k in (-3, 3):
-        spread(k)
+            carry(k, far if k < 0 else -far)
     for k in (-1, 1, -2, 2):
         z_arrival(k)
         spread(k)
+    spread(-3)
+    spread(3)
     x_arrivals(0)
-    for k in (-6, 6):
-        z_arrival(k)
-        if k < 0:
-            carry(k, 2)
-            carry(k, 1)
-        else:
-            carry(k, -1)
-    for k in (-6, 6):
-        spread(k)
+    z_arrival(-6)
+    carry(-6, 2)
+    carry(-6, 1)
+    z_arrival(6)
+    carry(6, -1)
+    for k in (-1, 1, -2, 2, -3, 3):
+        x_arrivals(k)
     for k in (-4, 4, -5, 5):
         z_arrival(k)
         spread(k)
-    for k in (-3, 3, -1, 1, -2, 2):
-        x_arrivals(k)
+    spread(-6)
+    spread(6)
+    far_arrival(0)
     for k in (-7, 7, -8):
         z_arrival(k)
         spread(k)
-    for k in (-6, 6, -4, 4, -5, 5, -7, 7, -8):
+    for k in (-4, 4, -5, 5, -6, 6):
         x_arrivals(k)
+    for k in (-1, 1, -2, 2, -3, 3):
+        far_arrival(k)
+    for k in (-7, 7, -8):
+        x_arrivals(k)
+    for k in (-4, 4, -5, 5, -6, 6, -7, 7, -8):
+        far_arrival(k)
     go(own.at[0, 63], hown.at[0], ys.at[0], yr.at[0], yp[0])
     go(own.at[0, 0], hown.at[1], ys.at[1], yr.at[1], yp[2])
     for n in range(64):
@@ -400,7 +422,7 @@
                 arrived(self.ref.at[self.rows(1 - k1), h * 1024:(h + 1) * 1024], self.rs.at[h, 3])
 
     s_out_w = Sum(dwo, dwo_ref, 32, eo1, ko1, eo2, eo_s, eo_r)
-    s_in_w = Sum(dwi, dwi_ref, 64, ei1, ki1, ei2, ei_s, ei_r)
+    s_in_w = Sum(dwi, dwi_sum, 64, ei1, ki1, ei2, ei_s, ei_r)
 
     acc[0:128, mine] = tn(gated_s[...], own[1].reshape(ROWS, HALF))
     acc[0:128, theirs] = tn(gated_s[...], oth[1].reshape(ROWS, HALF))
@@ -441,9 +463,12 @@
 
     near_rows = pl.ds(pl.multiple_of(zh * 256, 256), 256)
     g_f, g_r = gcat[near_rows, 0:256], gcat[near_rows, 256:512]
-    gin[0] = (nt(g_f, wcat[theirs, :]) + nt(g_r, wf[theirs, :])).astype(BF)
-    go(gin.at[0], rc, dc_s.at[0], dc_r.at[0], other)
-    gin[1] = (nt(g_f, wcat[mine, :]) + nt(g_r, wf[mine, :])).astype(BF)
+    for who in range(2):
+        for j in range(2):
+            c = pl.ds(pl.multiple_of((core if who else 1 - core) * HALF + j * 512, 512), 512)
+            gin[who, j] = (nt(g_f, wcat[c, :]) + nt(g_r, wf[c, :])).astype(BF)
+            if who == 0:
+                go(gin.at[0, j], rc.at[j], dc_s.at[j], dc_r.at[j], other)
     for k in (1, 2, 3):
         arrived(fx.at[k - 1], fx_r.at[k - 1])
     for k in range(8):
@@ -451,11 +476,13 @@
         f2[k] = (f1[x, r, :].astype(F32) + fx[0, r, :].astype(F32) + fx[1, r, :].astype(F32) + fx[2, r, :].astype(F32)).astype(BF)
     for k in range(1, 8):
         go(f2.at[lax.rem(zl + k, 8)], fz.at[k - 1], fz_s.at[k - 1], fz_r.at[k - 1], line(k))
-    arrived(rc, dc_r.at[0])
-    for k in range(4):
-        w1[k] = (gin[1, k * 64:(k + 1) * 64, :].astype(F32) + rc[k * 64:(k + 1) * 64, :].astype(F32)).astype(BF)
-    for k in (2, 1, 3):
-        go(w1.at[lax.rem(x + k, 4)], rx.at[k - 1], dx_s.at[k - 1], dx_r.at[k - 1], xp[k - 1])
+    for j in range(2):
+        arrived(rc.at[j], dc_r.at[j])
+        for k in range(4):
+            r = slice(k * 64, (k + 1) * 64)
+            w1[j, k] = (gin[1, j, r, :].astype(F32) + rc[j, r, :].astype(F32)).astype(BF)
+        for k in (2, 1, 3):
+            go(w1.at[j, lax.rem(x + k, 4)], rx.at[j, k - 1], dx_s.at[j, k - 1], dx_r.at[j, k - 1], xp[k - 1])
     s_out_w.third()
 
     both = jnp.concatenate([gcat[:, 0:128], gcat[:, 256:384]], axis=1)
@@ -475,44 +502,54 @@
     for k in range(3):
         go(fy, ry.at[k], fy_s.at[k], fy_r.at[k], yp[k])
     s_in_w.second()
-    for k in (1, 3, 2):
-        arrived(rx.at[k - 1], dx_r.at[k - 1])
-    for k in range(8):
-        r = slice(k * 8, (k + 1) * 8)
-        w2[k] = (w1[x, r, :].astype(F32) + rx[0, r, :].astype(F32) + rx[1, r, :].astype(F32) + rx[2, r, :].astype(F32)).astype(BF)
-    for k in (4, 5, 3, 6, 2, 7, 1):
-        go(w2.at[lax.rem(zl + k, 8)], rz.at[k - 1], dz_ss.at[k - 1], dz_rr.at[k - 1], line(k))
+    for j in range(2):
+        for k in (1, 3, 2):
+            arrived(rx.at[j, k - 1], dx_r.at[j, k - 1])
+        for k in range(8):
+            r = slice(k * 8, (k + 1) * 8)
+            w2[j, k] = (w1[j, x, r, :].astype(F32) + rx[j, 0, r, :].astype(F32) + rx[j, 1, r, :].astype(F32) + rx[j, 2, r, :].astype(F32)).astype(BF)
+        for k in (4, 5, 3, 6, 2, 7, 1):
+            go(w2.at[j, lax.rem(zl + k, 8)], rz.at[j, k - 1], dz_ss.at[j, k - 1], dz_rr.at[j, k - 1], line(k))
     for k in range(3):
         arrived(ry.at[k], fy_r.at[k])
     at = x * 8 + zl
-    fg_ref[core, at] = (fy[...] + ry[0] + ry[1] + ry[2]).astype(BF)
+    fg[core, at] = (fy[...] + ry[0] + ry[1] + ry[2]).astype(BF)
     for k in range(1, 8):
-        go(fg_ref.at[core, at], fg_ref.at[core, at], ga_s.at[k - 1], ga_r.at[k - 1], line(k))
+        go(fg.at[core, at], fg.at[core, at], ga_s.at[k - 1], ga_r.at[k - 1], line(k))
     s_in_w.third()
     for k in range(1, 8):
-        arrived(fg_ref.at[core, x * 8 + lax.rem(zl + 8 - k, 8)], ga_r.at[k - 1])
+        arrived(fg.at[core, x * 8 + lax.rem(zl + 8 - k, 8)], ga_r.at[k - 1])
     column = pl.ds(x * 8, 8)
     for k in (1, 2, 3):
-        go(fg_ref.at[core, column], fg_ref.at[core, column], ga_s.at[6 + k], ga_r.at[6 + k], xp[k - 1])
-    for k in range(1, 8):
-        arrived(rz.at[k - 1], dz_rr.at[k - 1])
-    hid = w2[zl].astype(F32)
-    for k in range(7):
-        hid = hid + rz[k].astype(F32)
-    hs[...] = hid.astype(BF)
-    go(hs, hr, dc_s.at[1], dc_r.at[1], other)
+        go(fg.at[core, column], fg.at[core, column], ga_s.at[6 + k], ga_r.at[6 + k], xp[k - 1])
+    for j in range(2):
+        for k in range(1, 8):
+            arrived(rz.at[j, k - 1], dz_rr.at[j, k - 1])
+        hid = w2[j, zl].astype(F32)
+        for k in range(7):
+            hid = hid + rz[j, k].astype(F32)
+        hs[:, j * 512:(j + 1) * 512] = hid.astype(BF)
+    go(hs, hr, dc_s.at[2], dc_r.at[2], other)
     s_in_w.fourth()
     for k in (1, 2, 3):
-        arrived(fg_ref.at[core, pl.ds(lax.rem(x + 4 - k, 4) * 8, 8)], ga_r.at[6 + k])
-    go(fg_ref.at[core], fg_ref.at[core], fc_s.at[1], fc_r.at[1], other)
-    arrived(hr, dc_r.at[1])
+        arrived(fg.at[core, pl.ds(lax.rem(x + 4 - k, 4) * 8, 8)], ga_r.at[6 + k])
+    go(fg.at[core], fg.at[core], fc_s.at[1], fc_r.at[1], other)
+    arrived(hr, dc_r.at[2])
     a, b = hs[...].astype(F32), hr[...].astype(F32)
     a, b = jnp.where(core == 0, a[0:4], a[4:8]), jnp.where(core == 0, b[0:4], b[4:8])
     hid_ref[:, 0:1024] = jnp.where(core == 0, a, b).astype(BF)
     hid_ref[:, 1024:2048] = jnp.where(core == 0, b, a).astype(BF)
-    arrived(fg_ref.at[1 - core], fc_r.at[1])
+    arrived(fg.at[1 - core], fc_r.at[1])
+    for k in range(2):
+        for m in range(8):
+            c = slice(k * HALF + m * 128, k * HALF + (m + 1) * 128)
+            for n in range(4):
+                shared_ref[n * 8:(n + 1) * 8, c] = fg[k, m * 4 + n]
     s_out_w.last()
     s_in_w.last()
+    for q in range(16):
+        r = slice(q * 128, (q + 1) * 128)
+        dwi_ref[r, :] = dwi_sum[:, r].astype(F32).T.astype(BF)
     for copy in pend:
         copy.wait_send()
 
@@ -530,35 +567,62 @@
     def out(*shape):
         return jax.ShapeDtypeStruct(shape, BF)
 
-    V = pl.BlockSpec(memory_space=pltpu.VMEM)
+    V, A = pl.BlockSpec(memory_space=pltpu.VMEM), pl.BlockSpec(memory_space=pl.ANY)
     scratch = [
+        bf(4, D), bf(4, D), bf(D, 128), bf(32, D), bf(1, D), f32(4, 64), bf(64, D), pltpu.SemaphoreType.DMA((7,)),
         bf(2, 4, HALF), f32(8, HALF), bf(2, 64, 8, HALF), bf(2, 64, 8, HALF), bf(2, 8, HALF), bf(2, 8, HALF),
         bf(D, 256), bf(D, 256), bf(128, D), f32(EXT, 128), f32(EXT, 128),
         f32(ROWS, 128), f32(ROWS, 128), f32(ROWS, 128), f32(ROWS, 128), bf(2, ROWS, 128), f32(ROWS, 128),
         f32(40, 128), f32(4, 40, 128), bf(ROWS, 128), f32(ROWS, 128), f32(ROWS, 128), bf(ROWS, 256), f32(2, 8, 128),
-        bf(ROWS, 512), f32(256, D), bf(128, D), bf(64, D), bf(2, 256, HALF), bf(256, HALF), bf(4, 64, HALF), bf(3, 64, HALF), bf(8, 8, HALF), bf(7, 8, HALF),
+        bf(ROWS, 512), f32(256, D), bf(128, D), bf(128, D), bf(64, D), bf(2, 32, 8, 128), bf(2, 2, 256, 512), bf(2, 256, 512), bf(2, 4, 64, 512), bf(2, 3, 64, 512), bf(2, 8, 8, 512), bf(2, 7, 8, 512),
         bf(8, HALF), bf(8, HALF),
         bf(2, 256, 128), bf(256, 128), bf(4, 64, 128), bf(3, 64, 128), bf(8, 8, 128), bf(7, 8, 128), f32(8, 128), f32(3, 8, 128),
         bf(2, 64, 1024), bf(2, 2, 64, 512), bf(2, 64, 512), bf(2, 32, 1024), bf(2, 2, 32, 512), bf(2, 32, 512),
-        *sems(2), *sems(16), *sems(3, 16), *sems(64), *sems(2), *sems(2), *sems(3), *sems(2),
-        *sems(2), *sems(3), *sems(7), *sems(2), *sems(3), *sems(7), *sems(3), *sems(10), *sems(2, 4), *sems(2, 4),
+        *sems(2), *sems(16), *sems(4, 16), *sems(64), *sems(2), *sems(2), *sems(3), *sems(2),
+        *sems(3), *sems(2, 3), *sems(2, 7), *sems(2), *sems(3), *sems(7), *sems(3), *sems(10), *sems(2, 4), *sems(2, 4),
     ]
     return pl.pallas_call(
         mixer_kernel,
-        out_shape=(out(4, D), out(128, D), out(64, D), out(2, 32, 8, 128)),
-        in_specs=[V] * 10, out_specs=[V] * 4, scratch_shapes=scratch,
+        out_shape=(out(4, D), out(D, 128), out(64, D), out(32, D)),
+        in_specs=[A] * 5 + [pl.BlockSpec(memory_space=pltpu.SMEM)] * 3 + [A] * 2, out_specs=[V] * 4, scratch_shapes=scratch,
         compiler_params=pltpu.CompilerParams(collective_id=0, has_side_effects=True, vmem_limit_bytes=56 << 20),
         name="mixer",
     )(*args)
 
 
+def widen_kernel(*refs):
+    sources, results, held, wide, sem_in, sem_out = refs[0:4], refs[4:8], refs[8:12], refs[12:16], refs[16], refs[17]
+    ins = [pltpu.make_async_copy(sources[k], held[k], sem_in.at[k]) for k in range(4)]
+    for copy in ins:
+        copy.start()
+    outs = []
+    for k in (1, 2, 3, 0):
+        ins[k].wait()
+        wide[k][...] = held[k][...].astype(wide[k].dtype)
+        outs.append(pltpu.make_async_copy(wide[k], results[k], sem_out.at[k]))
+        outs[-1].start()
+    for copy in outs:
+        copy.wait()
+
+
+def widen(*args):
+    A = pl.BlockSpec(memory_space=pl.ANY)
+    types = (BF, F32, F32, F32)
+    return pl.pallas_call(
+        widen_kernel,
+        out_shape=tuple(jax.ShapeDtypeStruct(a.shape, t) for a, t in zip(args, types)),
+        in_specs=[A] * 4, out_specs=[A] * 4,
+        scratch_shapes=[pltpu.VMEM(a.shape, BF) for a in args] + [pltpu.VMEM(a.shape, t) for a, t in zip(args, types)]
+        + [pltpu.SemaphoreType.DMA((4,))] * 2,
+        compiler_params=pltpu.CompilerParams(vmem_limit_bytes=56 << 20),
+        name="widen",
+    )(*args)
+
+
 def local(hidden, w_in, w_bc, w_dt, dt_bias, a_log, d_skip, conv_w, w_out, d_out):
-    one = (1, 1)
-    d_hidden, dwi, dwo, shared = mixer(
-        hidden, d_out, w_in, w_bc, w_dt, dt_bias.reshape(one), a_log.reshape(one), d_skip.reshape(one), conv_w, w_out
-    )
-    d_w_bc = shared.reshape(2, 8, 32, 128).transpose(0, 1, 3, 2).reshape(D, 2 * 16).astype(F32)
-    return (d_hidden, dwi.T.astype(F32), dwo.astype(F32), d_w_bc)
+    d_hidden, dwi, dwo, shared = mixer(hidden, d_out, w_in, w_bc.T, w_dt, dt_bias, a_log, d_skip, conv_w, w_out)
+    d_hidden, d_w_in, d_w_out, d_w_bc = widen(d_hidden, dwi, dwo, shared)
+    return (d_hidden, d_w_in, d_w_out, d_w_bc.T)
 
 
 def solution(mesh):

time: 104 us -> 94.9 us (0.913)
  local copies, waits for them, and re-layouts: 4.93 us -> 0 us
  other arithmetic: 1.98 us -> 0 us
  Pallas kernels: 94 us -> 92.1 us
    unnamed x10 -> x0, local copies, waits for them, and re-layouts: 4.77 us -> none
    convert_element_type x3 -> x0, other arithmetic: 1.98 us -> none  [the longest x2 1.96 us: local(): return (d_hidden, dwi.T.astype(F32), dwo.astype(F32), d_w_bc)]
    pallas_call x1 -> x2, Pallas kernels: 94 us -> 92.1 us  [the longest x1 89.7 us: mixer(): pl.pallas_call(mixer_kernel, out_shape=(out(4, D), out(D, 128), out(64, D...]
where the time goes in v3:
time: 94.9 us; the launch traced here: 94.7 us
  Pallas kernels  92.1 us (97%)
  between operations  2.58 us (3%)
    pallas_call x1, Pallas kernels, mixer(): pl.pallas_call(mixer_kernel, out_shape=(out(4, D), out(D, 128), out(64, D...  89.7 us
    pallas_call x1, Pallas kernels, widen(): pl.pallas_call(widen_kernel, out_shape=tuple((jax.ShapeDtypeStruct(a.shap...  2.42 us

profile of v3, /device:TPU:1, one launch (start us, length us, event | category | flops | bytes accessed | tf_op | source)
XLA Modules:
  0.0 94.7 jit_solution(12602610667042171375)
XLA Ops:
  2.6 89.7 %mixer.1 = (bf16[4,2048]{1,0:T(4,128)(2,1)}, bf16[2048,128]{1,0:T(8,128)(2,1)}, bf16[64,2048]{1,0:T(8,128)(2,1)}, bf16[32,2048]{1,0:T(8,128)(2,1)}) custom-call(bf16[4,2048]{1,0:T(4,128)(2,1)} %h_hbm.1, bf16[4,2048]{1,0:T(4,128)(2,1)} %g_hbm.1, bf16[2048,128]{1,0:T(8,128)(2,1)} %win_hbm.1, bf16[32,2048]{1,0:T(8,128)(2,1)} %bitcast.2, ...), custom_call_target="tpu_custom_call" | custom-call | tf_op jit(solution)/shard_map/mixer/pallas_call | solution.py:584
  92.3 2.4 %widen.1 = (bf16[4,2048]{1,0:T(4,128)(2,1)}, f32[2048,128]{1,0:T(8,128)}, f32[64,2048]{1,0:T(8,128)}, f32[32,2048]{1,0:T(8,128)}) custom-call(bf16[4,2048]{1,0:T(4,128)(2,1)} %get-tuple-element.12.refs_0_, bf16[2048,128]{1,0:T(8,128)(2,1)} %get-tuple-element.13.refs_1_, bf16[64,2048]{1,0:T(8,128)(2,1)} %get-tuple-element.14.refs_2_, ...), custom_call_target="tpu_custom_call" | custom-call | tf_op jit(solution)/shard_map/widen/pallas_call | solution.py:611

commit v4 on v3

--- a/solution.py
+++ b/solution.py
@@ -92,11 +92,11 @@
                  hid_ref, dwi_ref, dwo_ref, shared_ref,
                  h_ref, g_ref, win_ref, wbc_ref, wdt_ref, conv_ref, wout_ref, in_sem, swap, asm, own, oth, hown, hoth, wcat, wf, wo, x_scr, d_scr,
                  pre_s, z_s, dtr_s, gg_s, bc_s, cum_s, total_s, all_s, gated_s, dpre_s, dz_s, tail_s, edge_s,
-                 gcat, acc, dwi, dwi_sum, dwo, fg, gin, rc, w1, rx, w2, rz, hs, hr,
-                 fb, fc, f1, fx, f2, fz, fy, ry, ei1, ki1, ei2, eo1, ko1, eo2,
+                 gcat, acc, dwx, dwx_sum, dwz, dwz_sum, dwo, fg, gin, rc, w1, rx, w2, rz, hs, hr,
+                 fb, fc, f1, fx, f2, fz, ei1, ki1, ei2, ez1, kz1, ez2, eo1, ko1, eo2,
                  sw_s, sw_r, zs, zr, xs, xr, cs, cr, ys, yr, hs_s, hs_r, st_s, st_r, ed_s, ed_r,
-                 dc_s, dc_r, dx_s, dx_r, dz_ss, dz_rr, fc_s, fc_r, fx_s, fx_r, fz_s, fz_r, fy_s, fy_r, ga_s, ga_r,
-                 ei_s, ei_r, eo_s, eo_r):
+                 dc_s, dc_r, dx_s, dx_r, dz_ss, dz_rr, fc_s, fc_r, fx_s, fx_r, fz_s, fz_r, ga_s, ga_r,
+                 ei_s, ei_r, ez_s, ez_r, eo_s, eo_r):
     x, y, z, core = place()
     zh, zl = z // 8, z % 8
     bias, skip = bias_ref[0], skip_ref[0]
@@ -104,6 +104,8 @@
     other = dev(x, y, z, 1 - core)
     xp = [dev(lax.rem(x + k, 4), y, z, core) for k in (1, 2, 3)]
     yp = [dev(x, lax.rem(y + k, 4), z, core) for k in (1, 2, 3)]
+    steps = [(k // 4, k % 4) for k in range(1, 16)]
+    plane = [dev(lax.rem(x + i, 4), lax.rem(y + j, 4), z, core) for i, j in steps]
 
     def along(k):
         return dev(x, y, lax.rem(z + 16 + k, 16), core)
@@ -128,7 +130,7 @@
     for src, dst in ((h_hbm, h_ref), (g_hbm, g_ref), (wdt_hbm, wdt_ref), (conv_hbm, conv_ref), (wbc_hbm, wbc_ref), (win_hbm, win_ref), (wout_hbm, wout_ref)):
         loads.append(pltpu.make_async_copy(src, dst, in_sem.at[len(loads)]))
         loads[-1].start()
-    greet([other] + xp + yp + [along(k) for k in (-3, -2, -1, 1, 2, 3)] + [line(k) for k in range(1, 8)])
+    greet([other] + plane + [along(k) for k in (-3, -2, -1, 1, 2, 3)] + [line(k) for k in range(1, 8)])
 
     loads[0].wait()
     loads[1].wait()
@@ -251,9 +253,6 @@
     g_own, g_oth = own[1].reshape(ROWS, HALF), oth[1].reshape(ROWS, HALF)
     gg = nt(g_own, wo[:, mine]) + nt(g_oth, wo[:, theirs])
     gg_s[...] = gg
-    for j in range(2):
-        arrived(hown.at[j], yr.at[j])
-        go(hown.at[j], hoth.at[j], hs_s.at[j], hs_r.at[j], other)
     pf = nn(h_own, wcat[mine, :]) + nn(h_oth, wcat[theirs, :])
     pr = nn(h_own, wf[mine, :]) + nn(h_oth, wf[theirs, :])
     lanes = fwd_lanes((ROWS, 128))
@@ -270,6 +269,23 @@
     la = dt * rate
     dy = gg * (z2 * sigmoid(z2))
     for j in range(2):
+        arrived(hown.at[j], yr.at[j])
+        go(hown.at[j], hoth.at[j], hs_s.at[j], hs_r.at[j], other)
+    low = ones_where(iota((CH, CH), 0) >= iota((CH, CH), 1))
+    upp = ones_where(iota((CH, CH), 0) <= iota((CH, CH), 1))
+    lanes, lane1, lane16 = fwd_lanes((CH, 128)), fwd_lanes((1, 128)), fwd_lanes((16, 128))
+    ends, sts, ads, keeps = [], [], [], []
+    for c in range(2):
+        rows = slice(c * CH, (c + 1) * CH)
+        cum = jnp.where(lanes, exact_left(low, la[rows]), exact_left(upp, la[rows]))
+        cum_s[rows, :] = cum
+        end = jnp.where(lane1, cum[CH - 1:CH], cum[0:1])
+        ed = (jnp.exp(cum) * dy[rows]).astype(BF)
+        b0, b1 = bf[rows].astype(BF), br[rows].astype(BF)
+        ads.append(jnp.where(lane16, tn(b0, ed)[16:32], tn(b1, ed)[16:32]))
+        ends.append(end)
+        keeps.append((b0, b1, jnp.exp(end - cum)))
+    for j in range(2):
         arrived(hoth.at[j], hs_r.at[j])
     e_own, e_oth = hown[...].reshape(16, HALF), hoth[...].reshape(16, HALF)
     xf = nn(e_own, wcat[mine, 0:128]) + nn(e_oth, wcat[theirs, 0:128])
@@ -283,21 +299,10 @@
     pre_s[...] = pre
     u = dt * (pre * sigmoid(pre))
 
-    low = ones_where(iota((CH, CH), 0) >= iota((CH, CH), 1))
-    upp = ones_where(iota((CH, CH), 0) <= iota((CH, CH), 1))
-    lanes, lane1, lane16 = fwd_lanes((CH, 128)), fwd_lanes((1, 128)), fwd_lanes((16, 128))
-    ends, sts, ads = [], [], []
     for c in range(2):
-        rows = slice(c * CH, (c + 1) * CH)
-        cum = jnp.where(lanes, exact_left(low, la[rows]), exact_left(upp, la[rows]))
-        cum_s[rows, :] = cum
-        end = jnp.where(lane1, cum[CH - 1:CH], cum[0:1])
-        ru = (jnp.exp(end - cum) * u[rows]).astype(BF)
-        ed = (jnp.exp(cum) * dy[rows]).astype(BF)
-        b0, b1 = bf[rows].astype(BF), br[rows].astype(BF)
+        b0, b1, rem = keeps[c]
+        ru = (rem * u[c * CH:(c + 1) * CH]).astype(BF)
         sts.append(jnp.where(lane16, tn(b0, ru)[0:16], tn(b1, ru)[0:16]))
-        ads.append(jnp.where(lane16, tn(b0, ed)[16:32], tn(b1, ed)[16:32]))
-        ends.append(end)
     e0, e1 = jnp.exp(ends[0]), jnp.exp(ends[1])
     total_s[0:16, :] = jnp.where(lane16, e1 * sts[0] + sts[1], e0 * sts[1] + sts[0])
     total_s[16:32, :] = jnp.where(lane16, ads[0] + e0 * ads[1], ads[1] + e1 * ads[0])
@@ -422,17 +427,22 @@
                 arrived(self.ref.at[self.rows(1 - k1), h * 1024:(h + 1) * 1024], self.rs.at[h, 3])
 
     s_out_w = Sum(dwo, dwo_ref, 32, eo1, ko1, eo2, eo_s, eo_r)
-    s_in_w = Sum(dwi, dwi_sum, 64, ei1, ki1, ei2, ei_s, ei_r)
+    s_z = Sum(dwz, dwz_sum, 32, ez1, kz1, ez2, ez_s, ez_r)
+    s_x = Sum(dwx, dwx_sum, 32, ei1, ki1, ei2, ei_s, ei_r)
+
+    def both_strands(ref, lo):
+        for q in range(8):
+            c, back = slice(q * 256, (q + 1) * 256), slice((7 - q) * 256, (8 - q) * 256)
+            ref[:, c] = ((acc[lo:lo + 64, c] + nn(acc[lo + 64:lo + 128, back].astype(BF), flip)) * SCALING).astype(BF)
 
     acc[0:128, mine] = tn(gated_s[...], own[1].reshape(ROWS, HALF))
     acc[0:128, theirs] = tn(gated_s[...], oth[1].reshape(ROWS, HALF))
-    for q in range(8):
-        c, back = slice(q * 256, (q + 1) * 256), slice((7 - q) * 256, (8 - q) * 256)
-        dwo[:, c] = ((acc[0:64, c] + nn(acc[64:128, back].astype(BF), flip)) * SCALING).astype(BF)
+    both_strands(dwo, 0)
     s_out_w.first()
 
-    acc[:, mine] = tn(tail_s[...], own[0].reshape(ROWS, HALF))
-    acc[:, theirs] = tn(tail_s[...], oth[0].reshape(ROWS, HALF))
+    early = jnp.concatenate([tail_s[...], dz_s[...].astype(BF)], axis=1)
+    acc[:, mine] = tn(early, own[0].reshape(ROWS, HALF))
+    acc[:, theirs] = tn(early, oth[0].reshape(ROWS, HALF))
     for q in range(8):
         c, back = slice(q * 256, (q + 1) * 256), slice((7 - q) * 256, (8 - q) * 256)
         wb = ((acc[0:32, c] + nn(acc[128:160, back].astype(BF), flip)) * SCALING).astype(BF)
@@ -440,6 +450,8 @@
         fb[q // 4, m * 32:(m + 1) * 32, :] = wb[:, 0:128]
         fb[q // 4, (m + 1) * 32:(m + 2) * 32, :] = wb[:, 128:256]
     go(fb.at[1 - core], fc, fc_s.at[0], fc_r.at[0], other)
+    both_strands(dwz, 256)
+    s_z.first()
 
     d_scr[8:8 + ROWS, :] = dpre_s[...]
     for j in range(2):
@@ -455,10 +467,12 @@
     gcat[:, 256:384] = jnp.where(lanes, pltpu.roll(dx, 64, 1), dz).astype(BF)
 
     arrived(fc, fc_r.at[0])
-    for k in range(4):
-        f1[k] = (fb[core, k * 64:(k + 1) * 64, :].astype(F32) + fc[k * 64:(k + 1) * 64, :].astype(F32)).astype(BF)
-    for k in (1, 2, 3):
-        go(f1.at[lax.rem(x + k, 4)], fx.at[k - 1], fx_s.at[k - 1], fx_r.at[k - 1], xp[k - 1])
+    for k in range(16):
+        r = slice(k * 16, (k + 1) * 16)
+        f1[k] = (fb[core, r, :].astype(F32) + fc[r, :].astype(F32)).astype(BF)
+    for k in range(15):
+        i, j = steps[k]
+        go(f1.at[lax.rem(x + i, 4) * 4 + lax.rem(y + j, 4)], fx.at[k], fx_s.at[k], fx_r.at[k], plane[k])
     s_out_w.second()
 
     near_rows = pl.ds(pl.multiple_of(zh * 256, 256), 256)
@@ -469,13 +483,19 @@
             gin[who, j] = (nt(g_f, wcat[c, :]) + nt(g_r, wf[c, :])).astype(BF)
             if who == 0:
                 go(gin.at[0, j], rc.at[j], dc_s.at[j], dc_r.at[j], other)
-    for k in (1, 2, 3):
-        arrived(fx.at[k - 1], fx_r.at[k - 1])
-    for k in range(8):
-        r = slice(k * 8, (k + 1) * 8)
-        f2[k] = (f1[x, r, :].astype(F32) + fx[0, r, :].astype(F32) + fx[1, r, :].astype(F32) + fx[2, r, :].astype(F32)).astype(BF)
+    dxb = dx.astype(BF)
+    acc[0:128, mine] = tn(dxb, own[0].reshape(ROWS, HALF))
+    acc[0:128, theirs] = tn(dxb, oth[0].reshape(ROWS, HALF))
+    both_strands(dwx, 0)
+    s_x.first()
+    part = f1[x * 4 + y].astype(F32)
+    for k in range(15):
+        arrived(fx.at[k], fx_r.at[k])
+        part = part + fx[k].astype(F32)
+    f2[...] = part.astype(BF)
+    fz[zl] = part.astype(BF)
     for k in range(1, 8):
-        go(f2.at[lax.rem(zl + k, 8)], fz.at[k - 1], fz_s.at[k - 1], fz_r.at[k - 1], line(k))
+        go(f2, fz.at[zl], fz_s.at[k - 1], fz_r.at[k - 1], line(k))
     for j in range(2):
         arrived(rc.at[j], dc_r.at[j])
         for k in range(4):
@@ -484,24 +504,22 @@
         for k in (2, 1, 3):
             go(w1.at[j, lax.rem(x + k, 4)], rx.at[j, k - 1], dx_s.at[j, k - 1], dx_r.at[j, k - 1], xp[k - 1])
     s_out_w.third()
-
-    both = jnp.concatenate([gcat[:, 0:128], gcat[:, 256:384]], axis=1)
-    acc[:, mine] = tn(both, own[0].reshape(ROWS, HALF))
-    acc[:, theirs] = tn(both, oth[0].reshape(ROWS, HALF))
-    for q in range(8):
-        c, back = slice(q * 256, (q + 1) * 256), slice((7 - q) * 256, (8 - q) * 256)
-        dwi[:, c] = ((acc[0:128, c] + nn(acc[128:256, back].astype(BF), flip)) * SCALING).astype(BF)
-    s_in_w.first()
+    s_z.second()
+
+    s_x.second()
+    s_z.third()
     s_out_w.fourth()
     for k in range(1, 8):
-        arrived(fz.at[k - 1], fz_r.at[k - 1])
-    part = f2[zl].astype(F32)
-    for k in range(7):
+        arrived(fz.at[lax.rem(zl + 8 - k, 8)], fz_r.at[k - 1])
+    part = fz[0].astype(F32)
+    for k in range(1, 8):
         part = part + fz[k].astype(F32)
-    fy[...] = part
-    for k in range(3):
-        go(fy, ry.at[k], fy_s.at[k], fy_r.at[k], yp[k])
-    s_in_w.second()
+    at = x * 4 + y
+    fg[core, at] = part.astype(BF)
+    for k in range(15):
+        go(fg.at[core, at], fg.at[core, at], ga_s.at[k], ga_r.at[k], plane[k])
+    s_x.third()
+    s_z.fourth()
     for j in range(2):
         for k in (1, 3, 2):
             arrived(rx.at[j, k - 1], dx_r.at[j, k - 1])
@@ -510,18 +528,11 @@
             w2[j, k] = (w1[j, x, r, :].astype(F32) + rx[j, 0, r, :].astype(F32) + rx[j, 1, r, :].astype(F32) + rx[j, 2, r, :].astype(F32)).astype(BF)
         for k in (4, 5, 3, 6, 2, 7, 1):
             go(w2.at[j, lax.rem(zl + k, 8)], rz.at[j, k - 1], dz_ss.at[j, k - 1], dz_rr.at[j, k - 1], line(k))
-    for k in range(3):
-        arrived(ry.at[k], fy_r.at[k])
-    at = x * 8 + zl
-    fg[core, at] = (fy[...] + ry[0] + ry[1] + ry[2]).astype(BF)
-    for k in range(1, 8):
-        go(fg.at[core, at], fg.at[core, at], ga_s.at[k - 1], ga_r.at[k - 1], line(k))
-    s_in_w.third()
-    for k in range(1, 8):
-        arrived(fg.at[core, x * 8 + lax.rem(zl + 8 - k, 8)], ga_r.at[k - 1])
-    column = pl.ds(x * 8, 8)
-    for k in (1, 2, 3):
-        go(fg.at[core, column], fg.at[core, column], ga_s.at[6 + k], ga_r.at[6 + k], xp[k - 1])
+    s_x.fourth()
+    for k in range(15):
+        i, j = steps[k]
+        arrived(fg.at[core, lax.rem(x + 4 - i, 4) * 4 + lax.rem(y + 4 - j, 4)], ga_r.at[k])
+    go(fg.at[core], fg.at[core], fc_s.at[1], fc_r.at[1], other)
     for j in range(2):
         for k in range(1, 8):
             arrived(rz.at[j, k - 1], dz_rr.at[j, k - 1])
@@ -530,10 +541,6 @@
             hid = hid + rz[j, k].astype(F32)
         hs[:, j * 512:(j + 1) * 512] = hid.astype(BF)
     go(hs, hr, dc_s.at[2], dc_r.at[2], other)
-    s_in_w.fourth()
-    for k in (1, 2, 3):
-        arrived(fg.at[core, pl.ds(lax.rem(x + 4 - k, 4) * 8, 8)], ga_r.at[6 + k])
-    go(fg.at[core], fg.at[core], fc_s.at[1], fc_r.at[1], other)
     arrived(hr, dc_r.at[2])
     a, b = hs[...].astype(F32), hr[...].astype(F32)
     a, b = jnp.where(core == 0, a[0:4], a[4:8]), jnp.where(core == 0, b[0:4], b[4:8])
@@ -541,15 +548,16 @@
     hid_ref[:, 1024:2048] = jnp.where(core == 0, b, a).astype(BF)
     arrived(fg.at[1 - core], fc_r.at[1])
     for k in range(2):
-        for m in range(8):
-            c = slice(k * HALF + m * 128, k * HALF + (m + 1) * 128)
-            for n in range(4):
-                shared_ref[n * 8:(n + 1) * 8, c] = fg[k, m * 4 + n]
+        for m in range(16):
+            c = slice(k * HALF + (m // 2) * 128, k * HALF + (m // 2 + 1) * 128)
+            shared_ref[(m % 2) * 16:(m % 2 + 1) * 16, c] = fg[k, m]
     s_out_w.last()
-    s_in_w.last()
+    s_z.last()
+    s_x.last()
     for q in range(16):
         r = slice(q * 128, (q + 1) * 128)
-        dwi_ref[r, :] = dwi_sum[:, r].astype(F32).T.astype(BF)
+        turned = jnp.concatenate([dwx_sum[:, r].astype(F32), dwz_sum[:, r].astype(F32)], axis=0).T
+        dwi_ref[r, :] = turned.astype(BF)
     for copy in pend:
         copy.wait_send()
 
@@ -574,12 +582,12 @@
         bf(D, 256), bf(D, 256), bf(128, D), f32(EXT, 128), f32(EXT, 128),
         f32(ROWS, 128), f32(ROWS, 128), f32(ROWS, 128), f32(ROWS, 128), bf(2, ROWS, 128), f32(ROWS, 128),
         f32(40, 128), f32(4, 40, 128), bf(ROWS, 128), f32(ROWS, 128), f32(ROWS, 128), bf(ROWS, 256), f32(2, 8, 128),
-        bf(ROWS, 512), f32(256, D), bf(128, D), bf(128, D), bf(64, D), bf(2, 32, 8, 128), bf(2, 2, 256, 512), bf(2, 256, 512), bf(2, 4, 64, 512), bf(2, 3, 64, 512), bf(2, 8, 8, 512), bf(2, 7, 8, 512),
+        bf(ROWS, 512), f32(384, D), bf(64, D), bf(64, D), bf(64, D), bf(64, D), bf(64, D), bf(2, 16, 16, 128), bf(2, 2, 256, 512), bf(2, 256, 512), bf(2, 4, 64, 512), bf(2, 3, 64, 512), bf(2, 8, 8, 512), bf(2, 7, 8, 512),
         bf(8, HALF), bf(8, HALF),
-        bf(2, 256, 128), bf(256, 128), bf(4, 64, 128), bf(3, 64, 128), bf(8, 8, 128), bf(7, 8, 128), f32(8, 128), f32(3, 8, 128),
-        bf(2, 64, 1024), bf(2, 2, 64, 512), bf(2, 64, 512), bf(2, 32, 1024), bf(2, 2, 32, 512), bf(2, 32, 512),
+        bf(2, 256, 128), bf(256, 128), bf(16, 16, 128), bf(15, 16, 128), bf(16, 128), bf(8, 16, 128),
+        *[bf(2, 32, 1024), bf(2, 2, 32, 512), bf(2, 32, 512)] * 3,
         *sems(2), *sems(16), *sems(4, 16), *sems(64), *sems(2), *sems(2), *sems(3), *sems(2),
-        *sems(3), *sems(2, 3), *sems(2, 7), *sems(2), *sems(3), *sems(7), *sems(3), *sems(10), *sems(2, 4), *sems(2, 4),
+        *sems(3), *sems(2, 3), *sems(2, 7), *sems(2), *sems(15), *sems(7), *sems(15), *sems(2, 4), *sems(2, 4), *sems(2, 4),
     ]
     return pl.pallas_call(
         mixer_kernel,

time: 94.9 us -> 91.3 us (0.962)
  Pallas kernels: 92.1 us -> 88.5 us
    pallas_call x1, Pallas kernels: 89.7 us -> 86.1 us  [mixer(): pl.pallas_call(mixer_kernel, out_shape=(out(4, D), out(D, 128), out(64, D...]
where the time goes in v4:
time: 91.3 us; the launch traced here: 91.1 us
  Pallas kernels  88.5 us (97%)
  between operations  2.58 us (3%)
    pallas_call x1, Pallas kernels, mixer(): pl.pallas_call(mixer_kernel, out_shape=(out(4, D), out(D, 128), out(64, D...  86.1 us
    pallas_call x1, Pallas kernels, widen(): pl.pallas_call(widen_kernel, out_shape=tuple((jax.ShapeDtypeStruct(a.shap...  2.42 us

profile of v4, /device:TPU:1, one launch (start us, length us, event | category | flops | bytes accessed | tf_op | source)
XLA Modules:
  0.0 91.1 jit_solution(14234642447573562377)
XLA Ops:
  2.6 86.1 %mixer.1 = (bf16[4,2048]{1,0:T(4,128)(2,1)}, bf16[2048,128]{1,0:T(8,128)(2,1)}, bf16[64,2048]{1,0:T(8,128)(2,1)}, bf16[32,2048]{1,0:T(8,128)(2,1)}) custom-call(bf16[4,2048]{1,0:T(4,128)(2,1)} %h_hbm.1, bf16[4,2048]{1,0:T(4,128)(2,1)} %g_hbm.1, bf16[2048,128]{1,0:T(8,128)(2,1)} %win_hbm.1, bf16[32,2048]{1,0:T(8,128)(2,1)} %bitcast.2, ...), custom_call_target="tpu_custom_call" | custom-call | tf_op jit(solution)/shard_map/mixer/pallas_call | solution.py:592
  88.7 2.4 %widen.1 = (bf16[4,2048]{1,0:T(4,128)(2,1)}, f32[2048,128]{1,0:T(8,128)}, f32[64,2048]{1,0:T(8,128)}, f32[32,2048]{1,0:T(8,128)}) custom-call(bf16[4,2048]{1,0:T(4,128)(2,1)} %get-tuple-element.12.refs_0_, bf16[2048,128]{1,0:T(8,128)(2,1)} %get-tuple-element.13.refs_1_, bf16[64,2048]{1,0:T(8,128)(2,1)} %get-tuple-element.14.refs_2_, ...), custom_call_target="tpu_custom_call" | custom-call | tf_op jit(solution)/shard_map/widen/pallas_call | solution.py:619

commit v5 on v4

--- a/solution.py
+++ b/solution.py
@@ -478,8 +478,8 @@
     near_rows = pl.ds(pl.multiple_of(zh * 256, 256), 256)
     g_f, g_r = gcat[near_rows, 0:256], gcat[near_rows, 256:512]
     for who in range(2):
-        for j in range(2):
-            c = pl.ds(pl.multiple_of((core if who else 1 - core) * HALF + j * 512, 512), 512)
+        for j in range(4):
+            c = pl.ds(pl.multiple_of((core if who else 1 - core) * HALF + j * 256, 256), 256)
             gin[who, j] = (nt(g_f, wcat[c, :]) + nt(g_r, wf[c, :])).astype(BF)
             if who == 0:
                 go(gin.at[0, j], rc.at[j], dc_s.at[j], dc_r.at[j], other)
@@ -496,7 +496,7 @@
     fz[zl] = part.astype(BF)
     for k in range(1, 8):
         go(f2, fz.at[zl], fz_s.at[k - 1], fz_r.at[k - 1], line(k))
-    for j in range(2):
+    for j in range(4):
         arrived(rc.at[j], dc_r.at[j])
         for k in range(4):
             r = slice(k * 64, (k + 1) * 64)
@@ -520,7 +520,7 @@
         go(fg.at[core, at], fg.at[core, at], ga_s.at[k], ga_r.at[k], plane[k])
     s_x.third()
     s_z.fourth()
-    for j in range(2):
+    for j in range(4):
         for k in (1, 3, 2):
             arrived(rx.at[j, k - 1], dx_r.at[j, k - 1])
         for k in range(8):
@@ -533,15 +533,15 @@
         i, j = steps[k]
         arrived(fg.at[core, lax.rem(x + 4 - i, 4) * 4 + lax.rem(y + 4 - j, 4)], ga_r.at[k])
     go(fg.at[core], fg.at[core], fc_s.at[1], fc_r.at[1], other)
-    for j in range(2):
+    for j in range(4):
         for k in range(1, 8):
             arrived(rz.at[j, k - 1], dz_rr.at[j, k - 1])
         hid = w2[j, zl].astype(F32)
         for k in range(7):
             hid = hid + rz[j, k].astype(F32)
-        hs[:, j * 512:(j + 1) * 512] = hid.astype(BF)
-    go(hs, hr, dc_s.at[2], dc_r.at[2], other)
-    arrived(hr, dc_r.at[2])
+        hs[:, j * 256:(j + 1) * 256] = hid.astype(BF)
+    go(hs, hr, dc_s.at[4], dc_r.at[4], other)
+    arrived(hr, dc_r.at[4])
     a, b = hs[...].astype(F32), hr[...].astype(F32)
     a, b = jnp.where(core == 0, a[0:4], a[4:8]), jnp.where(core == 0, b[0:4], b[4:8])
     hid_ref[:, 0:1024] = jnp.where(core == 0, a, b).astype(BF)
@@ -582,12 +582,12 @@
         bf(D, 256), bf(D, 256), bf(128, D), f32(EXT, 128), f32(EXT, 128),
         f32(ROWS, 128), f32(ROWS, 128), f32(ROWS, 128), f32(ROWS, 128), bf(2, ROWS, 128), f32(ROWS, 128),
         f32(40, 128), f32(4, 40, 128), bf(ROWS, 128), f32(ROWS, 128), f32(ROWS, 128), bf(ROWS, 256), f32(2, 8, 128),
-        bf(ROWS, 512), f32(384, D), bf(64, D), bf(64, D), bf(64, D), bf(64, D), bf(64, D), bf(2, 16, 16, 128), bf(2, 2, 256, 512), bf(2, 256, 512), bf(2, 4, 64, 512), bf(2, 3, 64, 512), bf(2, 8, 8, 512), bf(2, 7, 8, 512),
+        bf(ROWS, 512), f32(384, D), bf(64, D), bf(64, D), bf(64, D), bf(64, D), bf(64, D), bf(2, 16, 16, 128), bf(2, 4, 256, 256), bf(4, 256, 256), bf(4, 4, 64, 256), bf(4, 3, 64, 256), bf(4, 8, 8, 256), bf(4, 7, 8, 256),
         bf(8, HALF), bf(8, HALF),
         bf(2, 256, 128), bf(256, 128), bf(16, 16, 128), bf(15, 16, 128), bf(16, 128), bf(8, 16, 128),
         *[bf(2, 32, 1024), bf(2, 2, 32, 512), bf(2, 32, 512)] * 3,
         *sems(2), *sems(16), *sems(4, 16), *sems(64), *sems(2), *sems(2), *sems(3), *sems(2),
-        *sems(3), *sems(2, 3), *sems(2, 7), *sems(2), *sems(15), *sems(7), *sems(15), *sems(2, 4), *sems(2, 4), *sems(2, 4),
+        *sems(5), *sems(4, 3), *sems(4, 7), *sems(2), *sems(15), *sems(7), *sems(15), *sems(2, 4), *sems(2, 4), *sems(2, 4),
     ]
     return pl.pallas_call(
         mixer_kernel,

time: 91.3 us -> 92.3 us (1.011)
  no operation moved by 1% of the time
where the time goes in v5:
time: 92.3 us; the launch traced here: 92.1 us
  Pallas kernels  89.4 us (97%)
  between operations  2.74 us (3%)
    pallas_call x1, Pallas kernels, mixer(): pl.pallas_call(mixer_kernel, out_shape=(out(4, D), out(D, 128), out(64, D...  87 us
    pallas_call x1, Pallas kernels, widen(): pl.pallas_call(widen_kernel, out_shape=tuple((jax.ShapeDtypeStruct(a.shap...  2.42 us

profile of v5, /device:TPU:1, one launch (start us, length us, event | category | flops | bytes accessed | tf_op | source)
XLA Modules:
  0.0 92.1 jit_solution(12812102425331848997)
XLA Ops:
  2.6 87.0 %mixer.1 = (bf16[4,2048]{1,0:T(4,128)(2,1)}, bf16[2048,128]{1,0:T(8,128)(2,1)}, bf16[64,2048]{1,0:T(8,128)(2,1)}, bf16[32,2048]{1,0:T(8,128)(2,1)}) custom-call(bf16[4,2048]{1,0:T(4,128)(2,1)} %h_hbm.1, bf16[4,2048]{1,0:T(4,128)(2,1)} %g_hbm.1, bf16[2048,128]{1,0:T(8,128)(2,1)} %win_hbm.1, bf16[32,2048]{1,0:T(8,128)(2,1)} %bitcast.2, ...), custom_call_target="tpu_custom_call" | custom-call | tf_op jit(solution)/shard_map/mixer/pallas_call | solution.py:592
  89.5 2.4 %widen.1 = (bf16[4,2048]{1,0:T(4,128)(2,1)}, f32[2048,128]{1,0:T(8,128)}, f32[64,2048]{1,0:T(8,128)}, f32[32,2048]{1,0:T(8,128)}) custom-call(bf16[4,2048]{1,0:T(4,128)(2,1)} %get-tuple-element.12.refs_0_, bf16[2048,128]{1,0:T(8,128)(2,1)} %get-tuple-element.13.refs_1_, bf16[64,2048]{1,0:T(8,128)(2,1)} %get-tuple-element.14.refs_2_, ...), custom_call_target="tpu_custom_call" | custom-call | tf_op jit(solution)/shard_map/widen/pallas_call | solution.py:619
